TPU v7x, 256 devices: a whole 4x4x8 slice. The times are simulated.
256 devices in a mesh: group: 16 (over y, x_hi, core), band: 16 (over z, x_lo).
Axes of the slice: x: 4 (x_hi: 2, x_lo: 2; x = x_hi * 2 + x_lo), y: 4, z: 8, core: 2. Of those that a mesh axis runs over, the one named last changes fastest.
Arguments:
- station_rows: int32 [16, 384, 128], P('group', 'band'), may hold values from 0 to 3
- station_lons: int32 [16, 384, 128], P('group', 'band'), may hold values from 0 to 1439
- station_obs: float32 [16, 384, 128], P('group', 'band'), may hold values from -6 to 6
- station_live: int32 [16, 384, 128], P('group', 'band'), may hold values 0 or 1
- block_band: int32 [16, 384, 1], P('group', 'band'), may hold values from 0 to 15; in each aligned block of 24 rows (0 to 23, 24 to 47, ..., all dimensions but the last counted through in order) at most 3 rows name the same one
- truth_field: float32 [16, 64, 1440], P('group', 'band'), may hold values from -6 to 6
- length_scales: float32 [4], replicated, may hold values from 1.5 to 6
- w_in: bfloat16 [3, 3, 32, 8], replicated, may hold values from -0.75 to 0.75
- w_down: bfloat16 [4, 4, 32, 32], replicated, may hold values from -0.25 to 0.25
- w_mid: bfloat16 [3, 3, 32, 32], replicated, may hold values from -0.375 to 0.375
- w_up: bfloat16 [3, 3, 32, 64], replicated, may hold values from -0.25 to 0.25
- w_head: bfloat16 [2, 32], replicated, may hold values from -1 to 1
Outputs:
- mean_field: float32 [16, 64, 1440], P('group', 'band')
- grad_in: float32 [3, 3, 32, 8], replicated
- grad_down: float32 [4, 4, 32, 32], replicated
- grad_mid: float32 [3, 3, 32, 32], replicated
- grad_up: float32 [3, 3, 32, 64], replicated
- grad_head: float32 [2, 32], replicated
Inputs may be any that keep to these rules, and one draw needn't show every extreme that they name: `block_band`: among the 24 blocks of one device no band is named by more than 3 blocks, and that number is reached.
All inputs are finite; a program needn't handle non-finite values. No bound on the sum of `station_live` on one device may be relied on, other than what follows from the above.
Results may differ from a plain program's by a relative error of at most 0.0025.
The roundings to bfloat16 on the way count: a program that leaves them out, or rounds other values in their place, can miss the bound.
Values may be sent and summed in bfloat16 or wider, within the bound.
A program may use at most 64 MiB of HBM per device.

v0:
```python
import functools

import jax
import jax.numpy as jnp
from jax import lax
from jax.experimental import pallas as pl
from jax.experimental.pallas import tpu as pltpu
from jax.sharding import PartitionSpec as P

MESH = pl.DeviceIdType.MESH
F32 = jnp.float32
BF16 = jnp.bfloat16
PHASES = (((1, 0), (3, -1)), ((0, 1), (2, 0)))
ROWS = 4
LON = 1440
HALF = 720
NBLK = 24
CAP = 3
LANES = 128
CELL = 120
SLABS = 12
CELLS = 92160.0
VMEM_LIMIT = 56 * 1024 * 1024


def dot(first, second):
    return lax.dot_general(first, second, (((1,), (0,)), ((), ())), preferred_element_type=F32)


def dot_t(first, second):
    return lax.dot_general(first, second, (((1,), (1,)), ((), ())), preferred_element_type=F32)


def iota(shape, dim):
    return lax.broadcasted_iota(jnp.int32, shape, dim)


def eye(size):
    return (iota((size, size), 0) == iota((size, size), 1)).astype(F32).astype(BF16)


def later(values, count):
    width = values.shape[-1]
    return jnp.concatenate([values[:, width - count :], values[:, : width - count]], axis=1)


def earlier(values, count):
    return jnp.concatenate([values[:, count:], values[:, :count]], axis=1)


def thirds(values):
    high = values.astype(BF16).astype(F32)
    rest = values - high
    middle = rest.astype(BF16).astype(F32)
    return high, middle, rest - middle


def sigmoid(values):
    return 1.0 / (1.0 + jnp.exp(-values))


def slope(values):
    squash = sigmoid(values)
    return squash * (1.0 + values * (1.0 - squash))


def as_scale(flag):
    return flag.astype(jnp.int32).astype(F32)


def step_kernel(
    n_group,
    n_band,
    rows_ref,
    lons_ref,
    obs_ref,
    live_ref,
    truth_ref,
    w_in,
    w_down,
    w_mid,
    w_up,
    w_head,
    band_ref,
    ell_ref,
    mean_out,
    in_out,
    down_out,
    mid_out,
    up_out,
    head_out,
    picked,
    outbox,
    inbox,
    hist,
    gauss,
    feats32,
    own_f,
    far_f,
    x_f,
    x_one,
    pre_one,
    x_two,
    pre_two,
    pre_three,
    x_three,
    pre_four,
    h_four,
    g_four,
    far_four,
    x_gfour,
    big_a,
    big_b,
    gj_one,
    g_three,
    far_three,
    x_gthree,
    g_two,
    far_two,
    x_gtwo,
    g_one,
    wb_in,
    wb_down,
    wb_mid,
    wb_up3,
    wb_up1,
    db_up,
    db_mid,
    db_down,
    grads,
    got,
    part,
    full,
    s_a,
    r_a,
    s_f,
    r_f,
    s_4,
    r_4,
    s_3,
    r_3,
    s_2,
    r_2,
    s_g1,
    r_g1,
    s_b,
    r_b,
    s_g2,
    r_g2,
):
    g = lax.axis_index("group")
    b = lax.axis_index("band")
    barrier = pltpu.get_barrier_semaphore()
    for k in range(1, n_group):
        pl.semaphore_signal(
            barrier, inc=1, device_id=(lax.rem(g + k, n_group), b), device_id_type=MESH
        )
    for k in range(1, n_band):
        pl.semaphore_signal(
            barrier, inc=1, device_id=(g, lax.rem(b + k, n_band)), device_id_type=MESH
        )

    def band_peer(k):
        return lax.rem(b + n_band + k, n_band)

    def group_peer(k):
        return lax.rem(g + n_group + k, n_group)

    sent = []
    chunk = 48 // n_group

    def send(source, target, send_sem, recv_sem, device):
        copy = pltpu.make_async_remote_copy(
            src_ref=source,
            dst_ref=target,
            send_sem=send_sem,
            recv_sem=recv_sem,
            device_id=device,
            device_id_type=MESH,
        )
        copy.start()
        sent.append(copy)

    def arrive(target, send_sem, recv_sem, device):
        pltpu.make_async_remote_copy(
            src_ref=target,
            dst_ref=target,
            send_sem=send_sem,
            recv_sem=recv_sem,
            device_id=device,
            device_id_type=MESH,
        ).wait_recv()

    slot_rows = iota((n_band * CAP, LANES), 0)
    slot_band, slot_place = slot_rows // CAP, slot_rows % CAP
    seen = jnp.zeros((n_band * CAP, LANES), jnp.int32)
    chosen = [jnp.zeros((n_band * CAP, LANES), F32) for _ in range(4)]
    for block in range(NBLK):
        mine = slot_band == band_ref[0, block, 0]
        here = jnp.logical_and(mine, seen == slot_place)
        fields = (
            rows_ref[0, block : block + 1, :].astype(F32),
            lons_ref[0, block : block + 1, :].astype(F32),
            obs_ref[0, block : block + 1, :],
            live_ref[0, block : block + 1, :].astype(F32),
        )
        chosen = [jnp.where(here, new, old) for new, old in zip(fields, chosen)]
        seen = seen + mine.astype(jnp.int32)
    for field in range(4):
        picked[field] = chosen[field]
    for q in range(n_band):
        for field in range(4):
            outbox[q, CAP * field : CAP * field + CAP, :] = picked[
                field, CAP * q : CAP * q + CAP, :
            ]

    pl.semaphore_wait(barrier, n_group + n_band - 2)
    for k in range(1, n_band):
        peer = band_peer(k)
        send(outbox.at[peer], inbox.at[b], s_a.at[k], r_a.at[b], (g, peer))
    inbox[b] = outbox[b]

    wide = (2 * LANES, 2 * LANES)
    row_id, col_id = iota(wide, 0), iota(wide, 1)
    base = (
        2 * (col_id % LANES) + col_id // LANES - row_id % LANES + CELL * (row_id // LANES)
    ).astype(F32)
    coefs = []
    for scale in range(4):
        ell = jnp.full((1, 2 * LANES), ell_ref[scale], F32)
        coefs.append(-0.5 / (ell * ell))

    def gauss_step(e, carry):
        gap = jnp.abs(base + (2 * CELL * e).astype(F32))
        gap = jnp.minimum(gap, LON - gap)
        square = gap * gap
        cols = pl.ds(pl.multiple_of(e * 2 * LANES, 2 * LANES), 2 * LANES)
        for scale in range(4):
            gauss[scale, :, cols] = jnp.exp(square * coefs[scale]).astype(BF16)
        return carry

    lax.fori_loop(0, SLABS // 2, gauss_step, 0)

    for ref in (wb_in, wb_down, wb_mid, wb_up3, wb_up1, db_up, db_mid, db_down):
        ref[...] = jnp.zeros_like(ref)
    turned_up = dot_t(eye(64), w_up[...].reshape(288, 64)).astype(BF16)
    turned_mid = dot_t(eye(32), w_mid[...].reshape(288, 32)).astype(BF16)
    turned_down = dot_t(eye(32), w_down[...].reshape(512, 32)).astype(BF16)
    for a in range(3):
        for t in range(3):
            block = w_in[a, t]
            for i in range(3):
                for p in range(2):
                    row, col = (2 * i + p) * 32, (i + a) * 32 + (t + p) * 8
                    wb_in[row : row + 32, col : col + 8] = block
            upper, lower = w_up[a, t, :, :32], w_up[a, t, :, 32:]
            at = ((2 - a) * 3 + 2 - t) * 32
            for i in range(2):
                for p in range(2):
                    row, col = (2 * i + p) * 32, (i + a) * 128 + (t + p) * 32
                    wb_up3[row : row + 32, col : col + 32] = upper
                    wb_up1[row : row + 32, col : col + 32] = lower
                    db_up[2 * row : 2 * row + 64, col : col + 32] = turned_up[:, at : at + 32]
                row, col = i * 32, (i + 2 * a) * 96 + t * 32
                wb_mid[row : row + 32, col : col + 32] = w_mid[a, t]
                db_mid[row : row + 32, col : col + 32] = turned_mid[:, at : at + 32]
    for a in range(4):
        for t in range(4):
            for m in range(2):
                col = (2 * m + a) * 128 + t * 32
                wb_down[m * 32 : m * 32 + 32, col : col + 32] = w_down[a, t]
    for m in range(2):
        for s in range(2):
            for p in range(2):
                row = ((2 * m + s) * 2 + p) * 32
                for a, up_down in PHASES[s]:
                    for t, left_right in PHASES[p]:
                        col = (m + up_down + 1) * 96 + (left_right + 1) * 32
                        at = (a * 4 + t) * 32
                        db_down[row : row + 32, col : col + 32] = turned_down[:, at : at + 32]
    head_row, head_col = iota((8, 256), 0), iota((8, 256), 1)
    matches = (head_col // 32) == (head_row % 4) * 2 + head_row // 4
    parts = []
    for k in range(2):
        line = jnp.concatenate([w_head[k : k + 1, :].astype(F32)] * 8, axis=1)
        parts.append(jnp.where(matches, line, 0.0))
    wb_head = jnp.concatenate(parts, axis=0).astype(BF16)
    db_head = dot_t(eye(256), wb_head).astype(BF16)

    weave = (col_id == 2 * (row_id % LANES) + row_id // LANES).astype(F32).astype(BF16)
    truth = jnp.concatenate([truth_ref[0], jnp.zeros((ROWS, LON), F32)], axis=0)
    truth = jnp.concatenate([truth, jnp.zeros((8, 96), F32)], axis=1)
    cuts = thirds(truth)
    lines = [cut[:, 256 * j : 256 * j + 256] for j in range(6) for cut in cuts]
    split = dot_t(jnp.concatenate(lines, axis=0).astype(BF16), weave)
    even, odd = [], []
    for j in range(6):
        one = split[24 * j : 24 * j + 8] + split[24 * j + 8 : 24 * j + 16]
        one = one + split[24 * j + 16 : 24 * j + 24]
        even.append(one[:, :LANES])
        odd.append(one[:, LANES:])
    truth_eo = jnp.concatenate(
        [jnp.concatenate(even, axis=1)[:ROWS], jnp.concatenate(odd, axis=1)[:ROWS]], axis=0
    )[:, :HALF]

    for k in range(1, n_band):
        peer = band_peer(-k)
        arrive(inbox.at[peer], s_a.at[k], r_a.at[peer], (g, peer))

    left_id = iota((32, LANES), 0)
    left_row = (left_id % 4).astype(F32)
    with_obs = (left_id // 4) % 2 == 1
    left_coef = jnp.zeros((32, LANES), F32)
    for scale in range(4):
        left_coef = jnp.where(left_id // 8 == scale, coefs[scale][:, :LANES], left_coef)
    lane_cell = iota((LANES, LANES), 0).astype(F32)
    hist[...] = jnp.zeros_like(hist)

    def hist_step(it, carry):
        lefts, rights = [], []
        for u in range(2):
            fields = inbox[2 * it + u]
            for slot in range(CAP):
                row = fields[slot : slot + 1]
                lon = fields[CAP + slot : CAP + slot + 1]
                seen_value = fields[2 * CAP + slot : 2 * CAP + slot + 1]
                alive = fields[3 * CAP + slot : 3 * CAP + slot + 1]
                slab = jnp.floor((lon + 0.5) * (1.0 / CELL))
                cell = lon - CELL * slab
                gap = left_row - row
                factor = jnp.where(with_obs, alive * seen_value, alive)
                left = factor * jnp.exp(gap * gap * left_coef)
                lefts.append(
                    jnp.concatenate(
                        [jnp.where(slab == float(h), left, 0.0) for h in range(SLABS)], axis=0
                    ).astype(BF16)
                )
                rights.append(jnp.where(lane_cell == cell, 1.0, 0.0).astype(BF16))
        hist[...] += dot_t(jnp.concatenate(lefts, axis=1), jnp.concatenate(rights, axis=1))
        return carry

    lax.fori_loop(0, n_band // 2, hist_step, 0)

    cuts = thirds(hist[...])
    for scale in range(4):
        lines = []
        for j in range(6):
            now, before = (2 * j) * 32 + 8 * scale, ((2 * j - 1) % SLABS) * 32 + 8 * scale
            for cut in cuts:
                lines.append(jnp.concatenate([cut[now : now + 8], cut[before : before + 8]], axis=1))
        spread = dot(jnp.concatenate(lines, axis=0).astype(BF16), gauss[scale])
        even, odd = [], []
        for j in range(6):
            total = None
            for e in range(6):
                at = 24 * ((j - e) % 6)
                for third in range(3):
                    piece = spread[at + 8 * third : at + 8 * third + 8, 256 * e : 256 * e + 256]
                    total = piece if total is None else total + piece
            even.append(total[:, :CELL])
            odd.append(total[:, LANES : LANES + CELL])
        for p, pieces in enumerate((even, odd)):
            sums = jnp.concatenate(pieces, axis=1)
            density, signal = sums[:4], sums[4:]
            base_p = 1.0 + density
            first, second = density / base_p, signal / base_p
            for r in range(ROWS):
                at = 8 * p + 2 * scale
                feats32[r, at : at + 1, :] = first[r : r + 1]
                feats32[r, at + 1 : at + 2, :] = second[r : r + 1]
    for r in range(ROWS):
        own_f[r] = feats32[r].astype(BF16)

    reach = (-2, -1, 1, 2)
    for n, k in enumerate(reach):
        send(own_f, far_f.at[3 - n], s_f.at[n], r_f.at[3 - n], (g, band_peer(k)))

    def feature_taps(source, scale):
        values = source.astype(F32) if scale is None else source.astype(F32) * scale
        even, odd = values[:8], values[8:]
        return jnp.concatenate([later(odd, 1), even, odd, earlier(even, 1)], axis=0).astype(BF16)

    for r in range(ROWS):
        x_f[8 + r] = feature_taps(own_f[r], None)
    for n, k in enumerate(reach):
        arrive(far_f.at[n], s_f.at[n], r_f.at[n], (g, band_peer(k)))
    for n, k in enumerate(reach):
        there = as_scale(jnp.logical_and(b + k >= 0, b + k < n_band))
        start = (0, 4, 12, 16)[n]
        for r in range(ROWS):
            x_f[start + r] = feature_taps(far_f[n, r], there)

    def one_step(it, carry):
        window = x_f[pl.ds(3 * it, 5)].reshape(160, HALF)
        value = dot(wb_in[...], window)
        for i in range(3):
            row = 3 * it + i
            place = ROWS * b + row - 7
            inside = as_scale(jnp.logical_and(place >= 0, place < ROWS * n_band))
            here = value[64 * i : 64 * i + 64]
            pre_one[row] = here
            hidden = (here * sigmoid(here) * inside).astype(BF16)
            even, odd = hidden[:32], hidden[32:]
            x_one[row, 0:32] = later(odd, 1)
            x_one[row, 32:64] = even
            x_one[row, 64:96] = odd
            x_one[row, 96:128] = earlier(even, 1)
        return carry

    lax.fori_loop(0, 6, one_step, 0)

    def two_step(it, carry):
        value = dot(wb_down[...], x_one[pl.ds(4 * it, 6)].reshape(768, HALF))
        for m in range(2):
            row = 2 * it + m
            place = 2 * b + row - 3
            inside = as_scale(jnp.logical_and(place >= 0, place < 2 * n_band))
            here = value[32 * m : 32 * m + 32]
            pre_two[row] = here
            hidden = (here * sigmoid(here) * inside).astype(BF16)
            x_two[row, 0:32] = later(hidden, 2)
            x_two[row, 32:64] = hidden
            x_two[row, 64:96] = earlier(hidden, 2)
        return carry

    lax.fori_loop(0, 4, two_step, 0)

    for it in range(2):
        value = dot(wb_mid[...], x_two[2 * it : 2 * it + 6].reshape(576, HALF))
        for m in range(2):
            row = 2 * it + m
            place = 2 * b + row - 1
            inside = as_scale(jnp.logical_and(place >= 0, place < 2 * n_band))
            here = value[32 * m : 32 * m + 32]
            pre_three[row] = here
            hidden = (here * sigmoid(here) * inside).astype(BF16)
            before, after = later(hidden, 1), earlier(hidden, 1)
            for target in ((0,), (1, 2), (3, 4), (5,))[row]:
                x_three[target, 0:32] = before
                x_three[target, 32:64] = hidden
                x_three[target, 64:96] = hidden
                x_three[target, 96:128] = after

    def four_step(it, carry):
        value = dot(wb_up3[...], x_three[pl.ds(2 * it, 4)].reshape(512, HALF))
        value = value + dot(wb_up1[...], x_one[pl.ds(2 * it + 6, 4)].reshape(512, HALF))
        rows = pl.ds(pl.multiple_of(128 * it, 128), 128)
        pre_four[rows, :] = value
        h_four[rows, :] = (value * sigmoid(value)).astype(BF16)
        return carry

    lax.fori_loop(0, 2, four_step, 0)

    head = dot(wb_head, h_four[...])
    mean, raw = head[:8], head[8:]
    noise = 0.1 + jnp.maximum(raw, 0.0) + jnp.log1p(jnp.exp(-jnp.abs(raw)))
    z = (mean - truth_eo) / noise
    per_cell = noise * CELLS
    g_head = jnp.concatenate(
        [z / per_cell, (1.0 - z * z) / per_cell * sigmoid(raw)], axis=0
    ).astype(BF16)

    def taps_of(target_ref, row, even, odd):
        target_ref[row, 0:32] = later(odd, 1)
        target_ref[row, 32:64] = even
        target_ref[row, 64:96] = odd
        target_ref[row, 96:128] = earlier(even, 1)

    back = dot(db_head, g_head)
    for i in (0, 3, 1, 2):
        rows = slice(64 * i, 64 * i + 64)
        g_four[i] = (back[rows] * slope(pre_four[rows, :])).astype(BF16)
        if i == 0:
            send(g_four.at[0], far_four.at[1], s_4.at[0], r_4.at[1], (g, band_peer(-1)))
        if i == 3:
            send(g_four.at[3], far_four.at[0], s_4.at[1], r_4.at[0], (g, band_peer(1)))

    mean_pad = jnp.concatenate([mean, jnp.zeros((8, 48), F32)], axis=1)
    cuts = thirds(mean_pad)
    lines = []
    for j in range(6):
        for cut in cuts:
            block = cut[:, LANES * j : LANES * j + LANES]
            swapped = jnp.concatenate([block[4:], block[:4]], axis=0)
            lines.append(jnp.concatenate([block, swapped], axis=1))
    woven = dot(jnp.concatenate(lines, axis=0).astype(BF16), weave)
    joined = []
    for j in range(6):
        one = woven[24 * j : 24 * j + 8] + woven[24 * j + 8 : 24 * j + 16]
        joined.append(one + woven[24 * j + 16 : 24 * j + 24])
    mean_out[0] = jnp.concatenate(joined, axis=1)[:ROWS, :LON]

    g_all = g_four[...].reshape(256, HALF)
    cross = dot_t(g_head, h_four[...])
    head_grad = []
    for k in range(2):
        line = jnp.sum(jnp.where(matches, cross[8 * k : 8 * k + 8], 0.0), axis=0, keepdims=True)
        total = line[:, 0:32]
        for n in range(1, 8):
            total = total + line[:, 32 * n : 32 * n + 32]
        head_grad.append(total)
    head_grad = jnp.concatenate(head_grad, axis=0)
    up_grads = []
    for ref, source in ((big_a, x_three[...]), (big_b, x_one[6:12])):
        ref[...] = dot_t(g_all, source.reshape(768, HALF))
        for a in range(3):
            total = None
            for i in range(4):
                for p in range(2):
                    row, col = (2 * i + p) * 32, (i + a) * 128 + p * 32
                    piece = ref[row : row + 32, col : col + 96]
                    total = piece if total is None else total + piece
            up_grads.append(total)

    for i in range(4):
        taps_of(x_gfour, i + 1, g_four[i, 0:32], g_four[i, 32:64])
    above = as_scale(b > 0)
    below = as_scale(b < n_band - 1)
    for n, (k, row, there) in enumerate(((-1, 0, above), (1, 5, below))):
        arrive(far_four.at[n], s_4.at[n], r_4.at[n], (g, band_peer(k)))
        value = (far_four[n].astype(F32) * there).astype(BF16)
        taps_of(x_gfour, row, value[:32], value[32:])

    for it in range(2):
        value = dot(db_up[...], x_gfour[2 * it : 2 * it + 4].reshape(512, HALF))
        pooled = None
        for s in range(2):
            for p in range(2):
                at = 128 * s + 64 * p
                rounded = value[at : at + 64].astype(BF16)
                gj_one[2 * it + s, 32 * p : 32 * p + 32] = rounded[32:]
                upper = rounded[:32].astype(F32)
                pooled = upper if pooled is None else pooled + upper
        g_three[it] = (pooled * slope(pre_three[it + 1])).astype(BF16)
    send(g_three, far_three.at[1], s_3.at[0], r_3.at[1], (g, band_peer(-1)))
    send(g_three, far_three.at[0], s_3.at[1], r_3.at[0], (g, band_peer(1)))

    def spread_taps(target_ref, row, value, count):
        target_ref[row, 0:32] = later(value, count)
        target_ref[row, 32:64] = value
        target_ref[row, 64:96] = earlier(value, count)

    cross = dot_t(g_three[...].reshape(64, HALF), x_two[1:7].reshape(576, HALF))
    mid_grads = [
        cross[0:32, 192 * a : 192 * a + 96] + cross[32:64, 192 * a + 96 : 192 * a + 192]
        for a in range(3)
    ]
    for m in range(2):
        spread_taps(x_gthree, 2 + m, g_three[m], 2)
    for n, (k, row, there) in enumerate(((-1, 0, above), (1, 4, below))):
        arrive(far_three.at[n], s_3.at[n], r_3.at[n], (g, band_peer(k)))
        for m in range(2):
            value = (far_three[n, m].astype(F32) * there).astype(BF16)
            spread_taps(x_gthree, row + m, value, 2)
    value = dot(db_mid[...], x_gthree[...].reshape(576, HALF))
    for m in range(2):
        g_two[m] = (value[32 * m : 32 * m + 32] * slope(pre_two[3 + m])).astype(BF16)
    send(g_two.at[0], far_two.at[1], s_2.at[0], r_2.at[1], (g, band_peer(-1)))
    send(g_two.at[1], far_two.at[0], s_2.at[1], r_2.at[0], (g, band_peer(1)))

    cross = dot_t(g_two[...].reshape(64, HALF), x_one[6:12].reshape(768, HALF))
    down_grads = [
        cross[0:32, 128 * a : 128 * a + 128] + cross[32:64, 128 * a + 256 : 128 * a + 384]
        for a in range(4)
    ]
    for m in range(2):
        spread_taps(x_gtwo, 1 + m, g_two[m], 1)
    for n, (k, row, there) in enumerate(((-1, 0, above), (1, 3, below))):
        arrive(far_two.at[n], s_2.at[n], r_2.at[n], (g, band_peer(k)))
        value = (far_two[n].astype(F32) * there).astype(BF16)
        spread_taps(x_gtwo, row, value, 1)
    value = dot(db_down[...], x_gtwo[...].reshape(384, HALF))
    for i in range(4):
        total = value[64 * i : 64 * i + 64] + gj_one[i].astype(F32)
        g_one[i] = (total * slope(pre_one[7 + i])).astype(BF16)
    cross = dot_t(g_one[...].reshape(256, HALF), x_f[7:13].reshape(192, HALF))
    in_grads = []
    for a in range(3):
        total = None
        for i in range(4):
            for p in range(2):
                row, col = (2 * i + p) * 32, (i + a) * 32 + p * 8
                piece = cross[row : row + 32, col : col + 24]
                total = piece if total is None else total + piece
        in_grads.append(total)

    blocks = list(down_grads)
    pieces = [grad[:, 32 * t : 32 * t + 32] for grad in mid_grads for t in range(3)]
    for n in range(6):
        blocks.append(jnp.concatenate([up_grads[n], pieces[n]], axis=1))
    blank = jnp.zeros((32, 8), F32)
    blocks.append(jnp.concatenate(pieces[6:9] + [in_grads[0], blank], axis=1))
    head_block = jnp.concatenate([head_grad, jnp.zeros((30, 32), F32)], axis=0)
    blocks.append(
        jnp.concatenate(
            [in_grads[1], blank, in_grads[2], blank, head_block, jnp.zeros((32, 32), F32)], axis=1
        )
    )
    for n, block in enumerate(blocks):
        grads[4 * n : 4 * n + 4] = block.reshape(4, 8, LANES)

    for k in range(1, n_group):
        peer = group_peer(k)
        send(grads.at[pl.ds(chunk * peer, chunk)], got.at[g], s_g1.at[k], r_g1.at[g], (peer, b))
    got[g] = grads[pl.ds(chunk * g, chunk)]
    for k in range(1, n_group):
        peer = group_peer(-k)
        arrive(got.at[peer], s_g1.at[k], r_g1.at[peer], (peer, b))
    total = got[0]
    for n in range(1, n_group):
        total = total + got[n]
    part[b] = total
    for k in range(1, n_band):
        peer = band_peer(k)
        send(part.at[b], part.at[b], s_b.at[k], r_b.at[b], (g, peer))
    for k in range(1, n_band):
        peer = band_peer(-k)
        arrive(part.at[peer], s_b.at[k], r_b.at[peer], (g, peer))
    total = part[0]
    for n in range(1, n_band):
        total = total + part[n]
    full[pl.ds(chunk * g, chunk)] = total
    for k in range(1, n_group):
        peer = group_peer(k)
        mine = full.at[pl.ds(chunk * g, chunk)]
        send(mine, mine, s_g2.at[k], r_g2.at[g], (peer, b))
    for k in range(1, n_group):
        peer = group_peer(-k)
        arrive(full.at[pl.ds(chunk * peer, chunk)], s_g2.at[k], r_g2.at[peer], (peer, b))

    def final(n):
        return full[4 * n : 4 * n + 4].reshape(32, LANES)

    last = [final(n) for n in range(12)]
    for a in range(4):
        for t in range(4):
            down_out[a, t] = last[a][:, 32 * t : 32 * t + 32]
    pieces = [last[4 + n][:, 96:128] for n in range(6)]
    pieces += [last[10][:, 32 * t : 32 * t + 32] for t in range(3)]
    wholes = (last[10][:, 96:120], last[11][:, 0:24], last[11][:, 32:56])
    for a in range(3):
        for t in range(3):
            up_out[a, t] = jnp.concatenate(
                [last[4 + a][:, 32 * t : 32 * t + 32], last[7 + a][:, 32 * t : 32 * t + 32]], axis=1
            )
            mid_out[a, t] = pieces[3 * a + t]
            in_out[a, t] = wholes[a][:, 8 * t : 8 * t + 8]
    head_out[...] = last[11][0:2, 64:96]
    for copy in sent:
        copy.wait_send()


def local(
    station_rows,
    station_lons,
    station_obs,
    station_live,
    block_band,
    truth_field,
    length_scales,
    w_in,
    w_down,
    w_mid,
    w_up,
    w_head,
):
    n_group, n_band = lax.axis_size("group"), lax.axis_size("band")
    vmem = pl.BlockSpec(memory_space=pltpu.VMEM)
    smem = pl.BlockSpec(memory_space=pltpu.SMEM)
    dma = pltpu.SemaphoreType.DMA

    def space(dtype, *shape):
        return pltpu.VMEM(shape, dtype)

    outs = (truth_field, w_in, w_down, w_mid, w_up, w_head)
    return pl.pallas_call(
        functools.partial(step_kernel, n_group, n_band),
        out_shape=[jax.ShapeDtypeStruct(out.shape, F32) for out in outs],
        in_specs=[vmem] * 10 + [smem] * 2,
        out_specs=[vmem] * 6,
        scratch_shapes=[
            space(F32, 4, n_band * CAP, LANES),
            space(F32, n_band, 4 * CAP, LANES),
            space(F32, n_band, 4 * CAP, LANES),
            space(F32, 32 * SLABS, LANES),
            space(BF16, 4, 2 * LANES, 6 * 2 * LANES),
            space(F32, ROWS, 16, HALF),
            space(BF16, ROWS, 16, HALF),
            space(BF16, 4, ROWS, 16, HALF),
            space(BF16, 20, 32, HALF),
            space(BF16, 18, 128, HALF),
            space(F32, 18, 64, HALF),
            space(BF16, 8, 96, HALF),
            space(F32, 8, 32, HALF),
            space(F32, 4, 32, HALF),
            space(BF16, 6, 128, HALF),
            space(F32, 256, HALF),
            space(BF16, 256, HALF),
            space(BF16, 4, 64, HALF),
            space(BF16, 2, 64, HALF),
            space(BF16, 6, 128, HALF),
            space(F32, 256, 768),
            space(F32, 256, 768),
            space(BF16, 4, 64, HALF),
            space(BF16, 2, 32, HALF),
            space(BF16, 2, 2, 32, HALF),
            space(BF16, 6, 96, HALF),
            space(BF16, 2, 32, HALF),
            space(BF16, 2, 32, HALF),
            space(BF16, 4, 96, HALF),
            space(BF16, 4, 64, HALF),
            space(BF16, 192, 160),
            space(BF16, 64, 768),
            space(BF16, 64, 576),
            space(BF16, 128, 512),
            space(BF16, 128, 512),
            space(BF16, 256, 512),
            space(BF16, 64, 576),
            space(BF16, 256, 384),
            space(F32, 48, 8, LANES),
            space(F32, n_group, 48 // n_group, 8, LANES),
            space(F32, n_band, 48 // n_group, 8, LANES),
            space(F32, 48, 8, LANES),
            dma((n_band,)),
            dma((n_band,)),
            dma((4,)),
            dma((4,)),
            dma((2,)),
            dma((2,)),
            dma((2,)),
            dma((2,)),
            dma((2,)),
            dma((2,)),
            dma((n_group,)),
            dma((n_group,)),
            dma((n_band,)),
            dma((n_band,)),
            dma((n_group,)),
            dma((n_group,)),
        ],
        compiler_params=pltpu.CompilerParams(
            collective_id=0, has_side_effects=True, vmem_limit_bytes=VMEM_LIMIT
        ),
    )(
        station_rows,
        station_lons,
        station_obs,
        station_live,
        truth_field,
        w_in,
        w_down,
        w_mid,
        w_up,
        w_head,
        block_band,
        length_scales,
    )


def solution(mesh):
    spread = P("group", "band", None)
    return jax.shard_map(
        local,
        mesh=mesh,
        in_specs=(spread,) * 6 + (P(),) * 6,
        out_specs=(spread,) + (P(),) * 5,
        check_vma=False,
    )
```

profile of v0, /device:TPU:1, one launch (start us, length us, event | category | flops | bytes accessed | tf_op | source)
XLA Modules:
  0.0 79.8 jit_solution(8452108788507897725)
XLA Ops:
  0.6 1.3 %copy.19.band_ref = s32[1,24,1]{2,1,0:T(8,128)} copy(s32[1,24,1]{1,2,0:T(1,128)} %param.16) | data formatting | bytes 192 | tf_op args[4]
  2.0 1.4 %copy.18.w_in = bf16[3,3,32,8]{3,2,1,0:T(8,128)(2,1)} copy(bf16[3,3,32,8]{2,3,1,0:T(8,128)(2,1)} %param.19) | data formatting | bytes 9216 | tf_op args[7]
  3.4 70.2 %shard_map.163 = (f32[1,4,1440]{2,1,0:T(4,128)}, f32[3,3,32,8]{3,2,1,0:T(8,128)}, f32[4,4,32,32]{3,2,1,0:T(8,128)}, f32[3,3,32,32]{3,2,1,0:T(8,128)}, f32[3,3,32,64]{3,2,1,0:T(8,128)}, /*index=5*/f32[2,32]{1,0:T(2,128)}) custom-call(s32[1,24,128]{2,1,0:T(8,128)} %rows_ref.1, s32[1,24,128]{2,1,0:T(8,128)} %lons_ref.1, f32[1,24,128]{2,1,0:T(8,128)} %obs_ref.1, ...), custom_call_target="tpu_custom_call" | custom-call | tf_op jit(solution)/shard_map/pallas_call | solution.py:676
  73.6 0.0 copy-start.2
  73.7 1.6 %copy.20 = f32[3,3,32,8]{2,3,1,0:T(8,128)} copy(f32[3,3,32,8]{3,2,1,0:T(8,128)} %get-tuple-element.7) | data formatting | bytes 18432 | tf_op jit(solution)/shard_map/pallas_call | solution.py:676
  75.3 0.0 copy-done.2
  75.3 0.6 copy.26
  75.9 0.0 copy-start.1
  75.9 1.7 %copy.27 = f32[4,4,32,32]{3,2,1,0:T(8,128)} copy(f32[4,4,32,32]{3,2,1,0:T(8,128)} %get-tuple-element.20) | data formatting | bytes 131072
  77.6 0.0 copy-done.1
  77.6 0.0 copy-start
  77.6 0.7 copy.28
  78.3 0.3 copy-done
  78.6 0.0 copy-start.3
  78.6 0.7 copy.29
  79.2 0.0 copy-done.3
  79.2 0.6 copy.30
Async XLA Ops:
  73.6 1.6 %copy-start.2 = (f32[1,4,1440]{2,1,0:T(4,128)S(1)}, f32[1,4,1440]{2,1,0:T(4,128)}, u32[]{:S(2)}) copy-start(f32[1,4,1440]{2,1,0:T(4,128)} %get-tuple-element.18) | copy-start | bytes 69124
  75.9 1.7 %copy-start.1 = (f32[3,3,32,32]{3,2,1,0:T(8,128)S(1)}, f32[3,3,32,32]{3,2,1,0:T(8,128)}, u32[]{:S(2)}) copy-start(f32[3,3,32,32]{3,2,1,0:T(8,128)} %get-tuple-element.21) | copy-start | bytes 110596
  77.6 1.0 %copy-start = (f32[3,3,32,64]{3,2,1,0:T(8,128)S(1)}, f32[3,3,32,64]{3,2,1,0:T(8,128)}, u32[]{:S(2)}) copy-start(f32[3,3,32,64]{3,2,1,0:T(8,128)} %get-tuple-element.22) | copy-start | bytes 221188
  78.6 0.7 copy-start.3
where the time goes:
time: 80.3 us; the launch traced here: 79.8 us
  Pallas kernels  70.2 us (87%)
  local copies, waits for them, and re-layouts  8.93 us (11%)
    pallas_call x1, Pallas kernels, local(): pl.pallas_call(functools.partial(step_kernel, n_group, n_band), out_shape...  70.2 us
    unnamed x15, local copies, waits for them, and re-layouts  7.29 us
    pallas_call x1, local copies, waits for them, and re-layouts, local(): pl.pallas_call(functools.partial(step_kernel, n_group, n_band), out_shape...  1.63 us

commit v1 on v0

--- a/solution.py
+++ b/solution.py
@@ -84,11 +84,9 @@
     band_ref,
     ell_ref,
     mean_out,
+    early_out,
+    late_out,
     in_out,
-    down_out,
-    mid_out,
-    up_out,
-    head_out,
     picked,
     outbox,
     inbox,
@@ -107,7 +105,8 @@
     pre_four,
     h_four,
     g_four,
-    far_four,
+    edge_out,
+    edge_in,
     x_gfour,
     big_a,
     big_b,
@@ -116,7 +115,6 @@
     far_three,
     x_gthree,
     g_two,
-    far_two,
     x_gtwo,
     g_one,
     wb_in,
@@ -127,26 +125,40 @@
     db_up,
     db_mid,
     db_down,
-    grads,
-    got,
-    part,
-    full,
+    early,
+    early_got,
+    early_part,
+    early_full,
+    late,
+    late_got,
+    late_part,
+    late_full,
+    in_got,
+    in_part,
     s_a,
     r_a,
     s_f,
     r_f,
-    s_4,
-    r_4,
+    s_t,
+    r_t,
     s_3,
     r_3,
-    s_2,
-    r_2,
-    s_g1,
-    r_g1,
-    s_b,
-    r_b,
-    s_g2,
-    r_g2,
+    s_e1,
+    r_e1,
+    s_e2,
+    r_e2,
+    s_e3,
+    r_e3,
+    s_l1,
+    r_l1,
+    s_l2,
+    r_l2,
+    s_l3,
+    r_l3,
+    s_i1,
+    r_i1,
+    s_i2,
+    r_i2,
 ):
     g = lax.axis_index("group")
     b = lax.axis_index("band")
@@ -167,7 +179,6 @@
         return lax.rem(g + n_group + k, n_group)
 
     sent = []
-    chunk = 48 // n_group
 
     def send(source, target, send_sem, recv_sem, device):
         copy = pltpu.make_async_remote_copy(
@@ -196,7 +207,7 @@
     seen = jnp.zeros((n_band * CAP, LANES), jnp.int32)
     chosen = [jnp.zeros((n_band * CAP, LANES), F32) for _ in range(4)]
     for block in range(NBLK):
-        mine = slot_band == band_ref[0, block, 0]
+        mine = slot_band == band_ref[0, 0, block]
         here = jnp.logical_and(mine, seen == slot_place)
         fields = (
             rows_ref[0, block : block + 1, :].astype(F32),
@@ -214,10 +225,14 @@
                 field, CAP * q : CAP * q + CAP, :
             ]
 
+    edge_out[0] = truth_ref[0, 0:1, :]
+    edge_out[1] = truth_ref[0, ROWS - 1 : ROWS, :]
     pl.semaphore_wait(barrier, n_group + n_band - 2)
     for k in range(1, n_band):
         peer = band_peer(k)
         send(outbox.at[peer], inbox.at[b], s_a.at[k], r_a.at[b], (g, peer))
+    send(edge_out.at[0], edge_in.at[1], s_t.at[0], r_t.at[1], (g, band_peer(-1)))
+    send(edge_out.at[1], edge_in.at[0], s_t.at[1], r_t.at[0], (g, band_peer(1)))
     inbox[b] = outbox[b]
 
     wide = (2 * LANES, 2 * LANES)
@@ -243,12 +258,14 @@
 
     for ref in (wb_in, wb_down, wb_mid, wb_up3, wb_up1, db_up, db_mid, db_down):
         ref[...] = jnp.zeros_like(ref)
+    turned_in = dot_t(eye(32), w_in[...].astype(F32).reshape(72, 32).astype(BF16)).astype(BF16)
     turned_up = dot_t(eye(64), w_up[...].reshape(288, 64)).astype(BF16)
     turned_mid = dot_t(eye(32), w_mid[...].reshape(288, 32)).astype(BF16)
     turned_down = dot_t(eye(32), w_down[...].reshape(512, 32)).astype(BF16)
     for a in range(3):
         for t in range(3):
-            block = w_in[a, t]
+            at = (a * 3 + t) * 8
+            block = turned_in[:, at : at + 8]
             for i in range(3):
                 for p in range(2):
                     row, col = (2 * i + p) * 32, (i + a) * 32 + (t + p) * 8
@@ -278,30 +295,17 @@
                         col = (m + up_down + 1) * 96 + (left_right + 1) * 32
                         at = (a * 4 + t) * 32
                         db_down[row : row + 32, col : col + 32] = turned_down[:, at : at + 32]
-    head_row, head_col = iota((8, 256), 0), iota((8, 256), 1)
-    matches = (head_col // 32) == (head_row % 4) * 2 + head_row // 4
+    head_row, head_col = iota((16, 384), 0), iota((16, 384), 1)
+    matches = (head_col // 32) == (head_row % 8) * 2 + head_row // 8
+    own_match = jnp.logical_and(matches, jnp.logical_and(head_col >= 64, head_col < 320))
     parts = []
     for k in range(2):
-        line = jnp.concatenate([w_head[k : k + 1, :].astype(F32)] * 8, axis=1)
+        line = jnp.concatenate([w_head[k : k + 1, :].astype(F32)] * 12, axis=1)
         parts.append(jnp.where(matches, line, 0.0))
     wb_head = jnp.concatenate(parts, axis=0).astype(BF16)
-    db_head = dot_t(eye(256), wb_head).astype(BF16)
+    db_head = dot_t(eye(384), wb_head).astype(BF16)
 
     weave = (col_id == 2 * (row_id % LANES) + row_id // LANES).astype(F32).astype(BF16)
-    truth = jnp.concatenate([truth_ref[0], jnp.zeros((ROWS, LON), F32)], axis=0)
-    truth = jnp.concatenate([truth, jnp.zeros((8, 96), F32)], axis=1)
-    cuts = thirds(truth)
-    lines = [cut[:, 256 * j : 256 * j + 256] for j in range(6) for cut in cuts]
-    split = dot_t(jnp.concatenate(lines, axis=0).astype(BF16), weave)
-    even, odd = [], []
-    for j in range(6):
-        one = split[24 * j : 24 * j + 8] + split[24 * j + 8 : 24 * j + 16]
-        one = one + split[24 * j + 16 : 24 * j + 24]
-        even.append(one[:, :LANES])
-        odd.append(one[:, LANES:])
-    truth_eo = jnp.concatenate(
-        [jnp.concatenate(even, axis=1)[:ROWS], jnp.concatenate(odd, axis=1)[:ROWS]], axis=0
-    )[:, :HALF]
 
     for k in range(1, n_band):
         peer = band_peer(-k)
@@ -382,6 +386,25 @@
 
     for r in range(ROWS):
         x_f[8 + r] = feature_taps(own_f[r], None)
+    for n, k in enumerate((-1, 1)):
+        arrive(edge_in.at[n], s_t.at[n], r_t.at[n], (g, band_peer(k)))
+    truth = jnp.concatenate(
+        [edge_in[0], truth_ref[0], edge_in[1], jnp.zeros((2, LON), F32)], axis=0
+    )
+    truth = jnp.concatenate([truth, jnp.zeros((8, 96), F32)], axis=1)
+    cuts = thirds(truth)
+    lines = [cut[:, 256 * j : 256 * j + 256] for j in range(6) for cut in cuts]
+    split = dot_t(jnp.concatenate(lines, axis=0).astype(BF16), weave)
+    even, odd = [], []
+    for j in range(6):
+        one = split[24 * j : 24 * j + 8] + split[24 * j + 8 : 24 * j + 16]
+        one = one + split[24 * j + 16 : 24 * j + 24]
+        even.append(one[:, :LANES])
+        odd.append(one[:, LANES:])
+    truth_eo = jnp.concatenate(
+        [jnp.concatenate(even, axis=1), jnp.concatenate(odd, axis=1)], axis=0
+    )[:, :HALF]
+
     for n, k in enumerate(reach):
         arrive(far_f.at[n], s_f.at[n], r_f.at[n], (g, band_peer(k)))
     for n, k in enumerate(reach):
@@ -435,7 +458,7 @@
             pre_three[row] = here
             hidden = (here * sigmoid(here) * inside).astype(BF16)
             before, after = later(hidden, 1), earlier(hidden, 1)
-            for target in ((0,), (1, 2), (3, 4), (5,))[row]:
+            for target in (2 * row, 2 * row + 1):
                 x_three[target, 0:32] = before
                 x_three[target, 32:64] = hidden
                 x_three[target, 64:96] = hidden
@@ -443,22 +466,25 @@
 
     def four_step(it, carry):
         value = dot(wb_up3[...], x_three[pl.ds(2 * it, 4)].reshape(512, HALF))
-        value = value + dot(wb_up1[...], x_one[pl.ds(2 * it + 6, 4)].reshape(512, HALF))
+        value = value + dot(wb_up1[...], x_one[pl.ds(2 * it + 5, 4)].reshape(512, HALF))
         rows = pl.ds(pl.multiple_of(128 * it, 128), 128)
         pre_four[rows, :] = value
         h_four[rows, :] = (value * sigmoid(value)).astype(BF16)
         return carry
 
-    lax.fori_loop(0, 2, four_step, 0)
+    lax.fori_loop(0, 3, four_step, 0)
 
     head = dot(wb_head, h_four[...])
-    mean, raw = head[:8], head[8:]
+    mean, raw = head[:16], head[16:]
     noise = 0.1 + jnp.maximum(raw, 0.0) + jnp.log1p(jnp.exp(-jnp.abs(raw)))
     z = (mean - truth_eo) / noise
     per_cell = noise * CELLS
-    g_head = jnp.concatenate(
-        [z / per_cell, (1.0 - z * z) / per_cell * sigmoid(raw)], axis=0
-    ).astype(BF16)
+    head_place = iota((16, HALF), 0) % 8 + ROWS * b - 1
+    on_grid = jnp.logical_and(head_place >= 0, head_place < ROWS * n_band)
+    on_grid = jnp.logical_and(on_grid, iota((16, HALF), 0) % 8 < 6)
+    g_mean = jnp.where(on_grid, z / per_cell, 0.0)
+    g_raw = jnp.where(on_grid, (1.0 - z * z) / per_cell * sigmoid(raw), 0.0)
+    g_head = jnp.concatenate([g_mean, g_raw], axis=0).astype(BF16)
 
     def taps_of(target_ref, row, even, odd):
         target_ref[row, 0:32] = later(odd, 1)
@@ -467,59 +493,11 @@
         target_ref[row, 96:128] = earlier(even, 1)
 
     back = dot(db_head, g_head)
-    for i in (0, 3, 1, 2):
+    for i in range(6):
         rows = slice(64 * i, 64 * i + 64)
-        g_four[i] = (back[rows] * slope(pre_four[rows, :])).astype(BF16)
-        if i == 0:
-            send(g_four.at[0], far_four.at[1], s_4.at[0], r_4.at[1], (g, band_peer(-1)))
-        if i == 3:
-            send(g_four.at[3], far_four.at[0], s_4.at[1], r_4.at[0], (g, band_peer(1)))
-
-    mean_pad = jnp.concatenate([mean, jnp.zeros((8, 48), F32)], axis=1)
-    cuts = thirds(mean_pad)
-    lines = []
-    for j in range(6):
-        for cut in cuts:
-            block = cut[:, LANES * j : LANES * j + LANES]
-            swapped = jnp.concatenate([block[4:], block[:4]], axis=0)
-            lines.append(jnp.concatenate([block, swapped], axis=1))
-    woven = dot(jnp.concatenate(lines, axis=0).astype(BF16), weave)
-    joined = []
-    for j in range(6):
-        one = woven[24 * j : 24 * j + 8] + woven[24 * j + 8 : 24 * j + 16]
-        joined.append(one + woven[24 * j + 16 : 24 * j + 24])
-    mean_out[0] = jnp.concatenate(joined, axis=1)[:ROWS, :LON]
-
-    g_all = g_four[...].reshape(256, HALF)
-    cross = dot_t(g_head, h_four[...])
-    head_grad = []
-    for k in range(2):
-        line = jnp.sum(jnp.where(matches, cross[8 * k : 8 * k + 8], 0.0), axis=0, keepdims=True)
-        total = line[:, 0:32]
-        for n in range(1, 8):
-            total = total + line[:, 32 * n : 32 * n + 32]
-        head_grad.append(total)
-    head_grad = jnp.concatenate(head_grad, axis=0)
-    up_grads = []
-    for ref, source in ((big_a, x_three[...]), (big_b, x_one[6:12])):
-        ref[...] = dot_t(g_all, source.reshape(768, HALF))
-        for a in range(3):
-            total = None
-            for i in range(4):
-                for p in range(2):
-                    row, col = (2 * i + p) * 32, (i + a) * 128 + p * 32
-                    piece = ref[row : row + 32, col : col + 96]
-                    total = piece if total is None else total + piece
-            up_grads.append(total)
-
-    for i in range(4):
-        taps_of(x_gfour, i + 1, g_four[i, 0:32], g_four[i, 32:64])
-    above = as_scale(b > 0)
-    below = as_scale(b < n_band - 1)
-    for n, (k, row, there) in enumerate(((-1, 0, above), (1, 5, below))):
-        arrive(far_four.at[n], s_4.at[n], r_4.at[n], (g, band_peer(k)))
-        value = (far_four[n].astype(F32) * there).astype(BF16)
-        taps_of(x_gfour, row, value[:32], value[32:])
+        value = (back[rows] * slope(pre_four[rows, :])).astype(BF16)
+        g_four[i] = value
+        taps_of(x_gfour, i, value[:32], value[32:])
 
     for it in range(2):
         value = dot(db_up[...], x_gfour[2 * it : 2 * it + 4].reshape(512, HALF))
@@ -532,122 +510,189 @@
                 upper = rounded[:32].astype(F32)
                 pooled = upper if pooled is None else pooled + upper
         g_three[it] = (pooled * slope(pre_three[it + 1])).astype(BF16)
-    send(g_three, far_three.at[1], s_3.at[0], r_3.at[1], (g, band_peer(-1)))
-    send(g_three, far_three.at[0], s_3.at[1], r_3.at[0], (g, band_peer(1)))
-
-    def spread_taps(target_ref, row, value, count):
-        target_ref[row, 0:32] = later(value, count)
-        target_ref[row, 32:64] = value
-        target_ref[row, 64:96] = earlier(value, count)
-
+    send(g_three, far_three.at[2], s_3.at[0], r_3.at[2], (g, band_peer(-1)))
+    send(g_three, far_three.at[1], s_3.at[1], r_3.at[1], (g, band_peer(1)))
+    send(g_three.at[0], far_three.at[3, 0], s_3.at[2], r_3.at[3], (g, band_peer(-2)))
+    send(g_three.at[1], far_three.at[0, 1], s_3.at[3], r_3.at[0], (g, band_peer(2)))
+
+    cuts = thirds(jnp.concatenate([mean, jnp.zeros((16, 48), F32)], axis=1))
+    lines = []
+    for j in range(6):
+        for cut in cuts:
+            block = cut[:, LANES * j : LANES * j + LANES]
+            lines.append(jnp.concatenate([block[:8], block[8:]], axis=1))
+    woven = dot(jnp.concatenate(lines, axis=0).astype(BF16), weave)
+    joined = []
+    for j in range(6):
+        one = woven[24 * j : 24 * j + 8] + woven[24 * j + 8 : 24 * j + 16]
+        joined.append(one + woven[24 * j + 16 : 24 * j + 24])
+    mean_out[0] = jnp.concatenate(joined, axis=1)[1 : 1 + ROWS, :LON]
+
+    g_all = g_four[1:5].reshape(256, HALF)
+    cross = dot_t(g_head, h_four[...])
+    head_grad = []
+    for k in range(2):
+        line = jnp.sum(
+            jnp.where(own_match, cross[16 * k : 16 * k + 16], 0.0), axis=0, keepdims=True
+        )
+        total = line[:, 0:32]
+        for n in range(1, 12):
+            total = total + line[:, 32 * n : 32 * n + 32]
+        head_grad.append(total)
+    head_grad = jnp.concatenate(head_grad + [jnp.zeros((30, 32), F32)], axis=0)
+    up_grads = []
+    for ref, source in ((big_a, x_three[1:7]), (big_b, x_one[6:12])):
+        ref[...] = dot_t(g_all, source.reshape(768, HALF))
+        for a in range(3):
+            total = None
+            for i in range(4):
+                for p in range(2):
+                    row, col = (2 * i + p) * 32, (i + a) * 128 + p * 32
+                    piece = ref[row : row + 32, col : col + 96]
+                    total = piece if total is None else total + piece
+            up_grads.append(total)
     cross = dot_t(g_three[...].reshape(64, HALF), x_two[1:7].reshape(576, HALF))
     mid_grads = [
         cross[0:32, 192 * a : 192 * a + 96] + cross[32:64, 192 * a + 96 : 192 * a + 192]
         for a in range(3)
     ]
+    pieces = [grad[:, 32 * t : 32 * t + 32] for grad in mid_grads for t in range(3)]
+    for n in range(6):
+        block = jnp.concatenate([up_grads[n], pieces[n]], axis=1)
+        early[4 * n : 4 * n + 4] = block.reshape(4, 8, LANES)
+    early[24:28] = jnp.concatenate(pieces[6:9] + [head_grad], axis=1).reshape(4, 8, LANES)
+    early[28:32] = jnp.zeros((4, 8, LANES), F32)
+
+    def scatter_group(source, size, target, send_sems, recv_sems):
+        for k in range(1, n_group):
+            peer = group_peer(k)
+            send(
+                source.at[pl.ds(size * peer, size)],
+                target.at[g],
+                send_sems.at[k],
+                recv_sems.at[g],
+                (peer, b),
+            )
+        target[g] = source[pl.ds(size * g, size)]
+
+    def spread_group(target, send_sems, recv_sems):
+        for k in range(1, n_group):
+            send(target.at[g], target.at[g], send_sems.at[k], recv_sems.at[g], (group_peer(k), b))
+
+    def spread_band(target, send_sems, recv_sems):
+        for k in range(1, n_band):
+            send(target.at[b], target.at[b], send_sems.at[k], recv_sems.at[b], (g, band_peer(k)))
+
+    def await_group(target, send_sems, recv_sems):
+        for k in range(1, n_group):
+            peer = group_peer(-k)
+            arrive(target.at[peer], send_sems.at[k], recv_sems.at[peer], (peer, b))
+
+    def await_band(target, send_sems, recv_sems):
+        for k in range(1, n_band):
+            peer = band_peer(-k)
+            arrive(target.at[peer], send_sems.at[k], recv_sems.at[peer], (g, peer))
+
+    def added(ref, count):
+        total = ref[0]
+        for n in range(1, count):
+            total = total + ref[n]
+        return total
+
+    early_size, late_size = 32 // n_group, 16 // n_group
+    scatter_group(early, early_size, early_got, s_e1, r_e1)
+
+    def spread_taps(target_ref, row, value, count):
+        target_ref[row, 0:32] = later(value, count)
+        target_ref[row, 32:64] = value
+        target_ref[row, 64:96] = earlier(value, count)
+
     for m in range(2):
-        spread_taps(x_gthree, 2 + m, g_three[m], 2)
-    for n, (k, row, there) in enumerate(((-1, 0, above), (1, 4, below))):
-        arrive(far_three.at[n], s_3.at[n], r_3.at[n], (g, band_peer(k)))
+        spread_taps(x_gthree, 3 + m, g_three[m], 2)
+    for n, k in ((1, -1), (2, 1), (0, -2), (3, 2)):
+        target = (far_three.at[0, 1], far_three.at[1], far_three.at[2], far_three.at[3, 0])[n]
+        arrive(target, s_3.at[n], r_3.at[n], (g, band_peer(k)))
+        there = as_scale(jnp.logical_and(b + k >= 0, b + k < n_band))
+        for m in ((1,), (0, 1), (0, 1), (0,))[n]:
+            value = (far_three[n, m].astype(F32) * there).astype(BF16)
+            spread_taps(x_gthree, 3 + 2 * k + m, value, 2)
+    for it in range(2):
+        value = dot(db_mid[...], x_gthree[2 * it : 2 * it + 6].reshape(576, HALF))
         for m in range(2):
-            value = (far_three[n, m].astype(F32) * there).astype(BF16)
-            spread_taps(x_gthree, row + m, value, 2)
-    value = dot(db_mid[...], x_gthree[...].reshape(576, HALF))
-    for m in range(2):
-        g_two[m] = (value[32 * m : 32 * m + 32] * slope(pre_two[3 + m])).astype(BF16)
-    send(g_two.at[0], far_two.at[1], s_2.at[0], r_2.at[1], (g, band_peer(-1)))
-    send(g_two.at[1], far_two.at[0], s_2.at[1], r_2.at[0], (g, band_peer(1)))
-
-    cross = dot_t(g_two[...].reshape(64, HALF), x_one[6:12].reshape(768, HALF))
-    down_grads = [
-        cross[0:32, 128 * a : 128 * a + 128] + cross[32:64, 128 * a + 256 : 128 * a + 384]
-        for a in range(4)
-    ]
-    for m in range(2):
-        spread_taps(x_gtwo, 1 + m, g_two[m], 1)
-    for n, (k, row, there) in enumerate(((-1, 0, above), (1, 3, below))):
-        arrive(far_two.at[n], s_2.at[n], r_2.at[n], (g, band_peer(k)))
-        value = (far_two[n].astype(F32) * there).astype(BF16)
-        spread_taps(x_gtwo, row, value, 1)
+            row = 2 * it + m
+            place = 2 * b + row - 1
+            inside = as_scale(jnp.logical_and(place >= 0, place < 2 * n_band))
+            here = value[32 * m : 32 * m + 32] * slope(pre_two[2 + row]) * inside
+            g_two[row] = here.astype(BF16)
+    cross = dot_t(g_two[1:3].reshape(64, HALF), x_one[6:12].reshape(768, HALF))
+    for a in range(4):
+        block = (
+            cross[0:32, 128 * a : 128 * a + 128] + cross[32:64, 128 * a + 256 : 128 * a + 384]
+        )
+        late[4 * a : 4 * a + 4] = block.reshape(4, 8, LANES)
+    scatter_group(late, late_size, late_got, s_l1, r_l1)
+    for m in range(4):
+        spread_taps(x_gtwo, m, g_two[m], 1)
     value = dot(db_down[...], x_gtwo[...].reshape(384, HALF))
     for i in range(4):
         total = value[64 * i : 64 * i + 64] + gj_one[i].astype(F32)
         g_one[i] = (total * slope(pre_one[7 + i])).astype(BF16)
-    cross = dot_t(g_one[...].reshape(256, HALF), x_f[7:13].reshape(192, HALF))
+    cross = dot_t(x_f[7:13].reshape(192, HALF), g_one[...].reshape(256, HALF))
     in_grads = []
     for a in range(3):
         total = None
         for i in range(4):
             for p in range(2):
-                row, col = (2 * i + p) * 32, (i + a) * 32 + p * 8
-                piece = cross[row : row + 32, col : col + 24]
+                row, col = (i + a) * 32 + p * 8, (2 * i + p) * 32
+                piece = cross[row : row + 24, col : col + 32]
                 total = piece if total is None else total + piece
         in_grads.append(total)
-
-    blocks = list(down_grads)
-    pieces = [grad[:, 32 * t : 32 * t + 32] for grad in mid_grads for t in range(3)]
-    for n in range(6):
-        blocks.append(jnp.concatenate([up_grads[n], pieces[n]], axis=1))
-    blank = jnp.zeros((32, 8), F32)
-    blocks.append(jnp.concatenate(pieces[6:9] + [in_grads[0], blank], axis=1))
-    head_block = jnp.concatenate([head_grad, jnp.zeros((30, 32), F32)], axis=0)
-    blocks.append(
-        jnp.concatenate(
-            [in_grads[1], blank, in_grads[2], blank, head_block, jnp.zeros((32, 32), F32)], axis=1
-        )
-    )
-    for n, block in enumerate(blocks):
-        grads[4 * n : 4 * n + 4] = block.reshape(4, 8, LANES)
-
-    for k in range(1, n_group):
-        peer = group_peer(k)
-        send(grads.at[pl.ds(chunk * peer, chunk)], got.at[g], s_g1.at[k], r_g1.at[g], (peer, b))
-    got[g] = grads[pl.ds(chunk * g, chunk)]
-    for k in range(1, n_group):
-        peer = group_peer(-k)
-        arrive(got.at[peer], s_g1.at[k], r_g1.at[peer], (peer, b))
-    total = got[0]
-    for n in range(1, n_group):
-        total = total + got[n]
-    part[b] = total
-    for k in range(1, n_band):
-        peer = band_peer(k)
-        send(part.at[b], part.at[b], s_b.at[k], r_b.at[b], (g, peer))
-    for k in range(1, n_band):
-        peer = band_peer(-k)
-        arrive(part.at[peer], s_b.at[k], r_b.at[peer], (g, peer))
-    total = part[0]
-    for n in range(1, n_band):
-        total = total + part[n]
-    full[pl.ds(chunk * g, chunk)] = total
-    for k in range(1, n_group):
-        peer = group_peer(k)
-        mine = full.at[pl.ds(chunk * g, chunk)]
-        send(mine, mine, s_g2.at[k], r_g2.at[g], (peer, b))
-    for k in range(1, n_group):
-        peer = group_peer(-k)
-        arrive(full.at[pl.ds(chunk * peer, chunk)], s_g2.at[k], r_g2.at[peer], (peer, b))
-
-    def final(n):
-        return full[4 * n : 4 * n + 4].reshape(32, LANES)
-
-    last = [final(n) for n in range(12)]
+    in_got[g] = jnp.concatenate(in_grads + [jnp.zeros((24, 32), F32)], axis=1)
+    spread_group(in_got, s_i1, r_i1)
+    await_group(early_got, s_e1, r_e1)
+    early_part[b] = added(early_got, n_group)
+    spread_band(early_part, s_e2, r_e2)
+    await_group(late_got, s_l1, r_l1)
+    late_part[b] = added(late_got, n_group)
+    spread_band(late_part, s_l2, r_l2)
+    await_group(in_got, s_i1, r_i1)
+    in_part[b] = added(in_got, n_group)
+    spread_band(in_part, s_i2, r_i2)
+    await_band(early_part, s_e2, r_e2)
+    early_full[g] = added(early_part, n_band)
+    spread_group(early_full, s_e3, r_e3)
+    await_band(late_part, s_l2, r_l2)
+    late_full[g] = added(late_part, n_band)
+    spread_group(late_full, s_l3, r_l3)
+    await_band(in_part, s_i2, r_i2)
+    in_out[...] = added(in_part, n_band)
+    await_group(early_full, s_e3, r_e3)
+    early_out[...] = early_full[...].reshape(32, 8, LANES)
+    await_group(late_full, s_l3, r_l3)
+    late_out[...] = late_full[...].reshape(16, 8, LANES)
+    for copy in sent:
+        copy.wait_send()
+
+
+def outputs_kernel(
+    mean_ref, early_ref, late_ref, in_ref, mean_out, in_out, down_out, mid_out, up_out, head_out
+):
+    mean_out[...] = mean_ref[...]
+    early = [early_ref[4 * n : 4 * n + 4].reshape(32, LANES) for n in range(7)]
+    pieces = [early[n][:, 96:128] for n in range(6)]
+    pieces += [early[6][:, 32 * t : 32 * t + 32] for t in range(3)]
     for a in range(4):
+        block = late_ref[4 * a : 4 * a + 4].reshape(32, LANES)
         for t in range(4):
-            down_out[a, t] = last[a][:, 32 * t : 32 * t + 32]
-    pieces = [last[4 + n][:, 96:128] for n in range(6)]
-    pieces += [last[10][:, 32 * t : 32 * t + 32] for t in range(3)]
-    wholes = (last[10][:, 96:120], last[11][:, 0:24], last[11][:, 32:56])
+            down_out[a, t] = block[:, 32 * t : 32 * t + 32]
     for a in range(3):
         for t in range(3):
             up_out[a, t] = jnp.concatenate(
-                [last[4 + a][:, 32 * t : 32 * t + 32], last[7 + a][:, 32 * t : 32 * t + 32]], axis=1
+                [early[a][:, 32 * t : 32 * t + 32], early[3 + a][:, 32 * t : 32 * t + 32]], axis=1
             )
             mid_out[a, t] = pieces[3 * a + t]
-            in_out[a, t] = wholes[a][:, 8 * t : 8 * t + 8]
-    head_out[...] = last[11][0:2, 64:96]
-    for copy in sent:
-        copy.wait_send()
+            in_out[a, t] = in_ref[8 * t : 8 * t + 8, 32 * a : 32 * a + 32]
+    head_out[...] = early[6][0:2, 96:128]
 
 
 def local(
@@ -672,12 +717,14 @@
     def space(dtype, *shape):
         return pltpu.VMEM(shape, dtype)
 
-    outs = (truth_field, w_in, w_down, w_mid, w_up, w_head)
-    return pl.pallas_call(
+    w_in = jnp.transpose(w_in, (0, 1, 3, 2))
+    early_size, late_size = 32 // n_group, 16 // n_group
+    raw = (truth_field.shape, (32, 8, LANES), (16, 8, LANES), (24, LANES))
+    summed = pl.pallas_call(
         functools.partial(step_kernel, n_group, n_band),
-        out_shape=[jax.ShapeDtypeStruct(out.shape, F32) for out in outs],
+        out_shape=[jax.ShapeDtypeStruct(shape, F32) for shape in raw],
         in_specs=[vmem] * 10 + [smem] * 2,
-        out_specs=[vmem] * 6,
+        out_specs=[vmem] * 4,
         scratch_shapes=[
             space(F32, 4, n_band * CAP, LANES),
             space(F32, n_band, 4 * CAP, LANES),
@@ -693,20 +740,20 @@
             space(BF16, 8, 96, HALF),
             space(F32, 8, 32, HALF),
             space(F32, 4, 32, HALF),
-            space(BF16, 6, 128, HALF),
-            space(F32, 256, HALF),
-            space(BF16, 256, HALF),
-            space(BF16, 4, 64, HALF),
-            space(BF16, 2, 64, HALF),
+            space(BF16, 8, 128, HALF),
+            space(F32, 384, HALF),
+            space(BF16, 384, HALF),
+            space(BF16, 6, 64, HALF),
+            space(F32, 2, 1, LON),
+            space(F32, 2, 1, LON),
             space(BF16, 6, 128, HALF),
             space(F32, 256, 768),
             space(F32, 256, 768),
             space(BF16, 4, 64, HALF),
             space(BF16, 2, 32, HALF),
-            space(BF16, 2, 2, 32, HALF),
-            space(BF16, 6, 96, HALF),
-            space(BF16, 2, 32, HALF),
-            space(BF16, 2, 32, HALF),
+            space(BF16, 4, 2, 32, HALF),
+            space(BF16, 8, 96, HALF),
+            space(BF16, 4, 32, HALF),
             space(BF16, 4, 96, HALF),
             space(BF16, 4, 64, HALF),
             space(BF16, 192, 160),
@@ -717,27 +764,27 @@
             space(BF16, 256, 512),
             space(BF16, 64, 576),
             space(BF16, 256, 384),
-            space(F32, 48, 8, LANES),
-            space(F32, n_group, 48 // n_group, 8, LANES),
-            space(F32, n_band, 48 // n_group, 8, LANES),
-            space(F32, 48, 8, LANES),
+            space(F32, 32, 8, LANES),
+            space(F32, n_group, early_size, 8, LANES),
+            space(F32, n_band, early_size, 8, LANES),
+            space(F32, n_group, early_size, 8, LANES),
+            space(F32, 16, 8, LANES),
+            space(F32, n_group, late_size, 8, LANES),
+            space(F32, n_band, late_size, 8, LANES),
+            space(F32, n_group, late_size, 8, LANES),
+            space(F32, n_group, 24, LANES),
+            space(F32, n_band, 24, LANES),
             dma((n_band,)),
             dma((n_band,)),
             dma((4,)),
             dma((4,)),
             dma((2,)),
             dma((2,)),
-            dma((2,)),
-            dma((2,)),
-            dma((2,)),
-            dma((2,)),
-            dma((n_group,)),
-            dma((n_group,)),
-            dma((n_band,)),
-            dma((n_band,)),
-            dma((n_group,)),
-            dma((n_group,)),
-        ],
+            dma((4,)),
+            dma((4,)),
+        ]
+        + [dma((count,)) for count in (n_group, n_band, n_group) * 2 for _ in range(2)]
+        + [dma((count,)) for count in (n_group, n_band) for _ in range(2)],
         compiler_params=pltpu.CompilerParams(
             collective_id=0, has_side_effects=True, vmem_limit_bytes=VMEM_LIMIT
         ),
@@ -752,9 +799,17 @@
         w_mid,
         w_up,
         w_head,
-        block_band,
+        jnp.transpose(block_band, (0, 2, 1)),
         length_scales,
     )
+    outs = (truth_field, w_in, w_down, w_mid, w_up, w_head)
+    mean, grad_in, grad_down, grad_mid, grad_up, grad_head = pl.pallas_call(
+        outputs_kernel,
+        out_shape=[jax.ShapeDtypeStruct(out.shape, F32) for out in outs],
+        in_specs=[vmem] * 4,
+        out_specs=[vmem] * 6,
+    )(*summed)
+    return mean, jnp.transpose(grad_in, (0, 1, 3, 2)), grad_down, grad_mid, grad_up, grad_head
 
 
 def solution(mesh):

time: 80.3 us -> 62.4 us (0.78)
  local copies, waits for them, and re-layouts: 8.93 us -> 0 us
  Pallas kernels: 70.2 us -> 61.6 us
    pallas_call x1, Pallas kernels: 70.2 us -> 59.7 us  [local(): pl.pallas_call(functools.partial(step_kernel, n_group, n_band), out_shape...]
    unnamed x15 -> x0, local copies, waits for them, and re-layouts: 7.29 us -> none
    pallas_call x0 -> x1, Pallas kernels: none -> 1.93 us  [local(): pl.pallas_call(outputs_kernel, out_shape=[jax.ShapeDtypeStruct(out.shape,...]
    pallas_call x1 -> x0, local copies, waits for them, and re-layouts: 1.63 us -> none  [local(): pl.pallas_call(functools.partial(step_kernel, n_group, n_band), out_shape...]
where the time goes in v1:
time: 62.4 us; the launch traced here: 62.2 us
  Pallas kernels  61.6 us (99%)
  between operations  0.64 us (1%)
    pallas_call x1, Pallas kernels, local(): pl.pallas_call(functools.partial(step_kernel, n_group, n_band), out_shape...  59.7 us
    pallas_call x1, Pallas kernels, local(): pl.pallas_call(outputs_kernel, out_shape=[jax.ShapeDtypeStruct(out.shape,...  1.93 us

profile of v1, /device:TPU:1, one launch (start us, length us, event | category | flops | bytes accessed | tf_op | source)
XLA Modules:
  0.0 62.2 jit_solution(12527011848807041004)
XLA Ops:
  0.6 59.7 %shard_map.163 = (f32[1,4,1440]{2,1,0:T(4,128)}, f32[32,8,128]{2,1,0:T(8,128)}, f32[16,8,128]{2,1,0:T(8,128)}, f32[24,128]{1,0:T(8,128)}) custom-call(s32[1,24,128]{2,1,0:T(8,128)} %rows_ref.1, s32[1,24,128]{2,1,0:T(8,128)} %lons_ref.1, f32[1,24,128]{2,1,0:T(8,128)} %obs_ref.1, s32[1,24,128]{2,1,0:T(8,128)} %live_ref.1, f32[1,4,1440]{2,1,0:T(4,128)} %truth_ref.1, ...), custom_call_target="tpu_custom_call" | custom-call | tf_op jit(solution)/shard_map/pallas_call | solution.py:723
  60.3 1.9 %shard_map.164 = (f32[1,4,1440]{2,1,0:T(4,128)}, f32[3,3,8,32]{3,2,1,0:T(8,128)}, f32[4,4,32,32]{3,2,1,0:T(8,128)}, f32[3,3,32,32]{3,2,1,0:T(8,128)}, f32[3,3,32,64]{3,2,1,0:T(8,128)}, /*index=5*/f32[2,32]{1,0:T(2,128)}) custom-call(f32[1,4,1440]{2,1,0:T(4,128)} %get-tuple-element.16.mean_ref, f32[32,8,128]{2,1,0:T(8,128)} %get-tuple-element.17.early_ref, ...), custom_call_target="tpu_custom_call" | custom-call | tf_op jit(solution)/shard_map/pallas_call | solution.py:806

commit v2 on v1

--- a/solution.py
+++ b/solution.py
@@ -56,7 +56,7 @@
 
 
 def sigmoid(values):
-    return 1.0 / (1.0 + jnp.exp(-values))
+    return 0.5 * jnp.tanh(0.5 * values) + 0.5
 
 
 def slope(values):
@@ -71,6 +71,22 @@
 def step_kernel(
     n_group,
     n_band,
+    rows_far,
+    lons_far,
+    obs_far,
+    live_far,
+    truth_far,
+    w_in_far,
+    w_down_far,
+    w_mid_far,
+    w_up_far,
+    w_head_far,
+    band_ref,
+    ell_ref,
+    mean_out,
+    early_out,
+    late_out,
+    in_out,
     rows_ref,
     lons_ref,
     obs_ref,
@@ -81,16 +97,10 @@
     w_mid,
     w_up,
     w_head,
-    band_ref,
-    ell_ref,
-    mean_out,
-    early_out,
-    late_out,
-    in_out,
+    s_in,
     picked,
     outbox,
     inbox,
-    hist,
     gauss,
     feats32,
     own_f,
@@ -202,6 +212,25 @@
             device_id_type=MESH,
         ).wait_recv()
 
+    fetches = []
+    pairs = (
+        (rows_far, rows_ref),
+        (lons_far, lons_ref),
+        (obs_far, obs_ref),
+        (live_far, live_ref),
+        (truth_far, truth_ref),
+        (w_in_far, w_in),
+        (w_down_far, w_down),
+        (w_mid_far, w_mid),
+        (w_up_far, w_up),
+        (w_head_far, w_head),
+    )
+    for n, (source, target) in enumerate(pairs):
+        fetch = pltpu.make_async_copy(source, target, s_in.at[n])
+        fetch.start()
+        fetches.append(fetch)
+    for fetch in fetches[:5]:
+        fetch.wait()
     slot_rows = iota((n_band * CAP, LANES), 0)
     slot_band, slot_place = slot_rows // CAP, slot_rows % CAP
     seen = jnp.zeros((n_band * CAP, LANES), jnp.int32)
@@ -256,6 +285,89 @@
 
     lax.fori_loop(0, SLABS // 2, gauss_step, 0)
 
+    weave = (col_id == 2 * (row_id % LANES) + row_id // LANES).astype(F32).astype(BF16)
+
+    left_id = iota((32, LANES), 0)
+    left_row = (left_id % 4).astype(F32)
+    with_obs = (left_id // 4) % 2 == 1
+    left_coef = jnp.zeros((32, LANES), F32)
+    for scale in range(4):
+        left_coef = jnp.where(left_id // 8 == scale, coefs[scale][:, :LANES], left_coef)
+    lane_cell = iota((LANES, LANES), 0).astype(F32)
+    counted = None
+    order = [0]
+    for k in range(1, n_band // 2):
+        order += [k, -k]
+    order.append(n_band // 2)
+    for quarter in range(4):
+        lefts, rights = [], []
+        for k in order[4 * quarter : 4 * quarter + 4]:
+            peer = band_peer(-k)
+            if k:
+                arrive(inbox.at[peer], s_a.at[k % n_band], r_a.at[peer], (g, peer))
+            fields = inbox[peer]
+            for slot in range(CAP):
+                row = fields[slot : slot + 1]
+                lon = fields[CAP + slot : CAP + slot + 1]
+                seen_value = fields[2 * CAP + slot : 2 * CAP + slot + 1]
+                alive = fields[3 * CAP + slot : 3 * CAP + slot + 1]
+                slab = jnp.floor((lon + 0.5) * (1.0 / CELL))
+                cell = lon - CELL * slab
+                gap = left_row - row
+                factor = jnp.where(with_obs, alive * seen_value, alive)
+                left = factor * jnp.exp(gap * gap * left_coef)
+                lefts.append(
+                    jnp.concatenate(
+                        [jnp.where(slab == float(h), left, 0.0) for h in range(SLABS)], axis=0
+                    ).astype(BF16)
+                )
+                rights.append(jnp.where(lane_cell == cell, 1.0, 0.0).astype(BF16))
+        more = dot_t(jnp.concatenate(lefts, axis=1), jnp.concatenate(rights, axis=1))
+        counted = more if counted is None else counted + more
+
+    cuts = thirds(counted)
+    for scale in range(4):
+        lines = []
+        for j in range(6):
+            now, before = (2 * j) * 32 + 8 * scale, ((2 * j - 1) % SLABS) * 32 + 8 * scale
+            for cut in cuts:
+                lines.append(jnp.concatenate([cut[now : now + 8], cut[before : before + 8]], axis=1))
+        spread = dot(jnp.concatenate(lines, axis=0).astype(BF16), gauss[scale])
+        even, odd = [], []
+        for j in range(6):
+            total = None
+            for e in range(6):
+                at = 24 * ((j - e) % 6)
+                for third in range(3):
+                    piece = spread[at + 8 * third : at + 8 * third + 8, 256 * e : 256 * e + 256]
+                    total = piece if total is None else total + piece
+            even.append(total[:, :CELL])
+            odd.append(total[:, LANES : LANES + CELL])
+        for p, pieces in enumerate((even, odd)):
+            sums = jnp.concatenate(pieces, axis=1)
+            density, signal = sums[:4], sums[4:]
+            base_p = 1.0 + density
+            first, second = density / base_p, signal / base_p
+            for r in range(ROWS):
+                at = 8 * p + 2 * scale
+                feats32[r, at : at + 1, :] = first[r : r + 1]
+                feats32[r, at + 1 : at + 2, :] = second[r : r + 1]
+    for r in range(ROWS):
+        own_f[r] = feats32[r].astype(BF16)
+
+    reach = (-2, -1, 1, 2)
+    for n, k in enumerate(reach):
+        send(own_f, far_f.at[3 - n], s_f.at[n], r_f.at[3 - n], (g, band_peer(k)))
+
+    def feature_taps(source, scale):
+        values = source.astype(F32) if scale is None else source.astype(F32) * scale
+        even, odd = values[:8], values[8:]
+        return jnp.concatenate([later(odd, 1), even, odd, earlier(even, 1)], axis=0).astype(BF16)
+
+    for r in range(ROWS):
+        x_f[8 + r] = feature_taps(own_f[r], None)
+    for fetch in fetches[5:]:
+        fetch.wait()
     for ref in (wb_in, wb_down, wb_mid, wb_up3, wb_up1, db_up, db_mid, db_down):
         ref[...] = jnp.zeros_like(ref)
     turned_in = dot_t(eye(32), w_in[...].astype(F32).reshape(72, 32).astype(BF16)).astype(BF16)
@@ -305,87 +417,6 @@
     wb_head = jnp.concatenate(parts, axis=0).astype(BF16)
     db_head = dot_t(eye(384), wb_head).astype(BF16)
 
-    weave = (col_id == 2 * (row_id % LANES) + row_id // LANES).astype(F32).astype(BF16)
-
-    for k in range(1, n_band):
-        peer = band_peer(-k)
-        arrive(inbox.at[peer], s_a.at[k], r_a.at[peer], (g, peer))
-
-    left_id = iota((32, LANES), 0)
-    left_row = (left_id % 4).astype(F32)
-    with_obs = (left_id // 4) % 2 == 1
-    left_coef = jnp.zeros((32, LANES), F32)
-    for scale in range(4):
-        left_coef = jnp.where(left_id // 8 == scale, coefs[scale][:, :LANES], left_coef)
-    lane_cell = iota((LANES, LANES), 0).astype(F32)
-    hist[...] = jnp.zeros_like(hist)
-
-    def hist_step(it, carry):
-        lefts, rights = [], []
-        for u in range(2):
-            fields = inbox[2 * it + u]
-            for slot in range(CAP):
-                row = fields[slot : slot + 1]
-                lon = fields[CAP + slot : CAP + slot + 1]
-                seen_value = fields[2 * CAP + slot : 2 * CAP + slot + 1]
-                alive = fields[3 * CAP + slot : 3 * CAP + slot + 1]
-                slab = jnp.floor((lon + 0.5) * (1.0 / CELL))
-                cell = lon - CELL * slab
-                gap = left_row - row
-                factor = jnp.where(with_obs, alive * seen_value, alive)
-                left = factor * jnp.exp(gap * gap * left_coef)
-                lefts.append(
-                    jnp.concatenate(
-                        [jnp.where(slab == float(h), left, 0.0) for h in range(SLABS)], axis=0
-                    ).astype(BF16)
-                )
-                rights.append(jnp.where(lane_cell == cell, 1.0, 0.0).astype(BF16))
-        hist[...] += dot_t(jnp.concatenate(lefts, axis=1), jnp.concatenate(rights, axis=1))
-        return carry
-
-    lax.fori_loop(0, n_band // 2, hist_step, 0)
-
-    cuts = thirds(hist[...])
-    for scale in range(4):
-        lines = []
-        for j in range(6):
-            now, before = (2 * j) * 32 + 8 * scale, ((2 * j - 1) % SLABS) * 32 + 8 * scale
-            for cut in cuts:
-                lines.append(jnp.concatenate([cut[now : now + 8], cut[before : before + 8]], axis=1))
-        spread = dot(jnp.concatenate(lines, axis=0).astype(BF16), gauss[scale])
-        even, odd = [], []
-        for j in range(6):
-            total = None
-            for e in range(6):
-                at = 24 * ((j - e) % 6)
-                for third in range(3):
-                    piece = spread[at + 8 * third : at + 8 * third + 8, 256 * e : 256 * e + 256]
-                    total = piece if total is None else total + piece
-            even.append(total[:, :CELL])
-            odd.append(total[:, LANES : LANES + CELL])
-        for p, pieces in enumerate((even, odd)):
-            sums = jnp.concatenate(pieces, axis=1)
-            density, signal = sums[:4], sums[4:]
-            base_p = 1.0 + density
-            first, second = density / base_p, signal / base_p
-            for r in range(ROWS):
-                at = 8 * p + 2 * scale
-                feats32[r, at : at + 1, :] = first[r : r + 1]
-                feats32[r, at + 1 : at + 2, :] = second[r : r + 1]
-    for r in range(ROWS):
-        own_f[r] = feats32[r].astype(BF16)
-
-    reach = (-2, -1, 1, 2)
-    for n, k in enumerate(reach):
-        send(own_f, far_f.at[3 - n], s_f.at[n], r_f.at[3 - n], (g, band_peer(k)))
-
-    def feature_taps(source, scale):
-        values = source.astype(F32) if scale is None else source.astype(F32) * scale
-        even, odd = values[:8], values[8:]
-        return jnp.concatenate([later(odd, 1), even, odd, earlier(even, 1)], axis=0).astype(BF16)
-
-    for r in range(ROWS):
-        x_f[8 + r] = feature_taps(own_f[r], None)
     for n, k in enumerate((-1, 1)):
         arrive(edge_in.at[n], s_t.at[n], r_t.at[n], (g, band_peer(k)))
     truth = jnp.concatenate(
@@ -430,7 +461,7 @@
             x_one[row, 96:128] = earlier(even, 1)
         return carry
 
-    lax.fori_loop(0, 6, one_step, 0)
+    lax.fori_loop(0, 6, one_step, 0, unroll=3)
 
     def two_step(it, carry):
         value = dot(wb_down[...], x_one[pl.ds(4 * it, 6)].reshape(768, HALF))
@@ -446,7 +477,7 @@
             x_two[row, 64:96] = earlier(hidden, 2)
         return carry
 
-    lax.fori_loop(0, 4, two_step, 0)
+    lax.fori_loop(0, 4, two_step, 0, unroll=True)
 
     for it in range(2):
         value = dot(wb_mid[...], x_two[2 * it : 2 * it + 6].reshape(576, HALF))
@@ -472,7 +503,7 @@
         h_four[rows, :] = (value * sigmoid(value)).astype(BF16)
         return carry
 
-    lax.fori_loop(0, 3, four_step, 0)
+    lax.fori_loop(0, 3, four_step, 0, unroll=True)
 
     head = dot(wb_head, h_four[...])
     mean, raw = head[:16], head[16:]
@@ -722,14 +753,29 @@
     raw = (truth_field.shape, (32, 8, LANES), (16, 8, LANES), (24, LANES))
     summed = pl.pallas_call(
         functools.partial(step_kernel, n_group, n_band),
-        out_shape=[jax.ShapeDtypeStruct(shape, F32) for shape in raw],
-        in_specs=[vmem] * 10 + [smem] * 2,
+        out_shape=[pltpu.VMEM(shape, F32) for shape in raw],
+        in_specs=[pl.BlockSpec(memory_space=pl.ANY)] * 10 + [smem] * 2,
         out_specs=[vmem] * 4,
         scratch_shapes=[
+            pltpu.VMEM(part.shape, part.dtype)
+            for part in (
+                station_rows,
+                station_lons,
+                station_obs,
+                station_live,
+                truth_field,
+                w_in,
+                w_down,
+                w_mid,
+                w_up,
+                w_head,
+            )
+        ]
+        + [
+            dma((10,)),
             space(F32, 4, n_band * CAP, LANES),
             space(F32, n_band, 4 * CAP, LANES),
             space(F32, n_band, 4 * CAP, LANES),
-            space(F32, 32 * SLABS, LANES),
             space(BF16, 4, 2 * LANES, 6 * 2 * LANES),
             space(F32, ROWS, 16, HALF),
             space(BF16, ROWS, 16, HALF),
@@ -808,7 +854,7 @@
         out_shape=[jax.ShapeDtypeStruct(out.shape, F32) for out in outs],
         in_specs=[vmem] * 4,
         out_specs=[vmem] * 6,
-    )(*summed)
+    )(*[pltpu.with_memory_space_constraint(part, pltpu.VMEM) for part in summed])
     return mean, jnp.transpose(grad_in, (0, 1, 3, 2)), grad_down, grad_mid, grad_up, grad_head
 
 

time: 62.4 us -> 57.6 us (0.923)
  Pallas kernels: 61.6 us -> 56.8 us
    pallas_call x1, Pallas kernels: 59.7 us -> 55.8 us  [local(): pl.pallas_call(functools.partial(step_kernel, n_group, n_band), out_shape...]
    pallas_call x1, Pallas kernels: 1.93 us -> 1.01 us  [local(): pl.pallas_call(outputs_kernel, out_shape=[jax.ShapeDtypeStruct(out.shape,...]
where the time goes in v2:
time: 57.6 us; the launch traced here: 57.5 us
  Pallas kernels  56.8 us (99%)
  between operations  0.64 us (1%)
    pallas_call x1, Pallas kernels, local(): pl.pallas_call(functools.partial(step_kernel, n_group, n_band), out_shape...  55.8 us

profile of v2, /device:TPU:1, one launch (start us, length us, event | category | flops | bytes accessed | tf_op | source)
XLA Modules:
  0.0 57.5 jit_solution(14904289368593450919)
XLA Ops:
  0.6 55.8 %shard_map.163 = (f32[1,4,1440]{2,1,0:T(4,128)S(1)}, f32[32,8,128]{2,1,0:T(8,128)S(1)}, f32[16,8,128]{2,1,0:T(8,128)S(1)}, f32[24,128]{1,0:T(8,128)S(1)}) custom-call(s32[1,24,128]{2,1,0:T(8,128)} %rows_far.1, s32[1,24,128]{2,1,0:T(8,128)} %lons_far.1, f32[1,24,128]{2,1,0:T(8,128)} %obs_far.1, s32[1,24,128]{2,1,0:T(8,128)} %live_far.1, ...), custom_call_target="tpu_custom_call" | custom-call | tf_op jit(solution)/shard_map/pallas_call | solution.py:754
  56.4 1.0 %shard_map.164 = (f32[1,4,1440]{2,1,0:T(4,128)}, f32[3,3,8,32]{3,2,1,0:T(8,128)}, f32[4,4,32,32]{3,2,1,0:T(8,128)}, f32[3,3,32,32]{3,2,1,0:T(8,128)}, f32[3,3,32,64]{3,2,1,0:T(8,128)}, /*index=5*/f32[2,32]{1,0:T(2,128)}) custom-call(f32[1,4,1440]{2,1,0:T(4,128)S(1)} %get-tuple-element.16.mean_ref, f32[32,8,128]{2,1,0:T(8,128)S(1)} %get-tuple-element.17.early_ref, ...), custom_call_target="tpu_custom_call" | custom-call | tf_op jit(solution)/shard_map/pallas_call | solution.py:852

commit v3 on v2

--- a/solution.py
+++ b/solution.py
@@ -541,23 +541,14 @@
                 upper = rounded[:32].astype(F32)
                 pooled = upper if pooled is None else pooled + upper
         g_three[it] = (pooled * slope(pre_three[it + 1])).astype(BF16)
-    send(g_three, far_three.at[2], s_3.at[0], r_3.at[2], (g, band_peer(-1)))
-    send(g_three, far_three.at[1], s_3.at[1], r_3.at[1], (g, band_peer(1)))
-    send(g_three.at[0], far_three.at[3, 0], s_3.at[2], r_3.at[3], (g, band_peer(-2)))
-    send(g_three.at[1], far_three.at[0, 1], s_3.at[3], r_3.at[0], (g, band_peer(2)))
-
-    cuts = thirds(jnp.concatenate([mean, jnp.zeros((16, 48), F32)], axis=1))
-    lines = []
-    for j in range(6):
-        for cut in cuts:
-            block = cut[:, LANES * j : LANES * j + LANES]
-            lines.append(jnp.concatenate([block[:8], block[8:]], axis=1))
-    woven = dot(jnp.concatenate(lines, axis=0).astype(BF16), weave)
-    joined = []
-    for j in range(6):
-        one = woven[24 * j : 24 * j + 8] + woven[24 * j + 8 : 24 * j + 16]
-        joined.append(one + woven[24 * j + 16 : 24 * j + 24])
-    mean_out[0] = jnp.concatenate(joined, axis=1)[1 : 1 + ROWS, :LON]
+        for slot, k in ((2, -1), (1, 1), (3, -2) if it == 0 else (0, 2)):
+            send(
+                g_three.at[it],
+                far_three.at[slot, it],
+                s_3.at[slot, it],
+                r_3.at[slot, it],
+                (g, band_peer(k)),
+            )
 
     g_all = g_four[1:5].reshape(256, HALF)
     cross = dot_t(g_head, h_four[...])
@@ -633,6 +624,19 @@
     early_size, late_size = 32 // n_group, 16 // n_group
     scatter_group(early, early_size, early_got, s_e1, r_e1)
 
+    cuts = thirds(jnp.concatenate([mean, jnp.zeros((16, 48), F32)], axis=1))
+    lines = []
+    for j in range(6):
+        for cut in cuts:
+            block = cut[:, LANES * j : LANES * j + LANES]
+            lines.append(jnp.concatenate([block[:8], block[8:]], axis=1))
+    woven = dot(jnp.concatenate(lines, axis=0).astype(BF16), weave)
+    joined = []
+    for j in range(6):
+        one = woven[24 * j : 24 * j + 8] + woven[24 * j + 8 : 24 * j + 16]
+        joined.append(one + woven[24 * j + 16 : 24 * j + 24])
+    mean_out[0] = jnp.concatenate(joined, axis=1)[1 : 1 + ROWS, :LON]
+
     def spread_taps(target_ref, row, value, count):
         target_ref[row, 0:32] = later(value, count)
         target_ref[row, 32:64] = value
@@ -640,13 +644,11 @@
 
     for m in range(2):
         spread_taps(x_gthree, 3 + m, g_three[m], 2)
-    for n, k in ((1, -1), (2, 1), (0, -2), (3, 2)):
-        target = (far_three.at[0, 1], far_three.at[1], far_three.at[2], far_three.at[3, 0])[n]
-        arrive(target, s_3.at[n], r_3.at[n], (g, band_peer(k)))
+    for n, k, m in ((1, -1, 0), (2, 1, 0), (3, 2, 0), (0, -2, 1), (1, -1, 1), (2, 1, 1)):
+        arrive(far_three.at[n, m], s_3.at[n, m], r_3.at[n, m], (g, band_peer(k)))
         there = as_scale(jnp.logical_and(b + k >= 0, b + k < n_band))
-        for m in ((1,), (0, 1), (0, 1), (0,))[n]:
-            value = (far_three[n, m].astype(F32) * there).astype(BF16)
-            spread_taps(x_gthree, 3 + 2 * k + m, value, 2)
+        value = (far_three[n, m].astype(F32) * there).astype(BF16)
+        spread_taps(x_gthree, 3 + 2 * k + m, value, 2)
     for it in range(2):
         value = dot(db_mid[...], x_gthree[2 * it : 2 * it + 6].reshape(576, HALF))
         for m in range(2):
@@ -662,6 +664,9 @@
         )
         late[4 * a : 4 * a + 4] = block.reshape(4, 8, LANES)
     scatter_group(late, late_size, late_got, s_l1, r_l1)
+    await_group(early_got, s_e1, r_e1)
+    early_part[b] = added(early_got, n_group)
+    spread_band(early_part, s_e2, r_e2)
     for m in range(4):
         spread_taps(x_gtwo, m, g_two[m], 1)
     value = dot(db_down[...], x_gtwo[...].reshape(384, HALF))
@@ -678,25 +683,28 @@
                 piece = cross[row : row + 24, col : col + 32]
                 total = piece if total is None else total + piece
         in_grads.append(total)
-    in_got[g] = jnp.concatenate(in_grads + [jnp.zeros((24, 32), F32)], axis=1)
-    spread_group(in_got, s_i1, r_i1)
-    await_group(early_got, s_e1, r_e1)
-    early_part[b] = added(early_got, n_group)
-    spread_band(early_part, s_e2, r_e2)
+    in_got[b] = jnp.concatenate(
+        [
+            jnp.concatenate([grad[:18] for grad in in_grads], axis=1),
+            jnp.concatenate([grad[18:] for grad in in_grads], axis=0),
+        ],
+        axis=1,
+    )
+    spread_band(in_got, s_i1, r_i1)
     await_group(late_got, s_l1, r_l1)
     late_part[b] = added(late_got, n_group)
     spread_band(late_part, s_l2, r_l2)
-    await_group(in_got, s_i1, r_i1)
-    in_part[b] = added(in_got, n_group)
-    spread_band(in_part, s_i2, r_i2)
+    await_band(in_got, s_i1, r_i1)
+    in_part[g] = added(in_got, n_band)
+    spread_group(in_part, s_i2, r_i2)
     await_band(early_part, s_e2, r_e2)
     early_full[g] = added(early_part, n_band)
     spread_group(early_full, s_e3, r_e3)
     await_band(late_part, s_l2, r_l2)
     late_full[g] = added(late_part, n_band)
     spread_group(late_full, s_l3, r_l3)
-    await_band(in_part, s_i2, r_i2)
-    in_out[...] = added(in_part, n_band)
+    await_group(in_part, s_i2, r_i2)
+    in_out[...] = added(in_part, n_group)
     await_group(early_full, s_e3, r_e3)
     early_out[...] = early_full[...].reshape(32, 8, LANES)
     await_group(late_full, s_l3, r_l3)
@@ -722,8 +730,14 @@
                 [early[a][:, 32 * t : 32 * t + 32], early[3 + a][:, 32 * t : 32 * t + 32]], axis=1
             )
             mid_out[a, t] = pieces[3 * a + t]
-            in_out[a, t] = in_ref[8 * t : 8 * t + 8, 32 * a : 32 * a + 32]
     head_out[...] = early[6][0:2, 96:128]
+    packed = in_ref[...]
+    for a in range(3):
+        whole = jnp.concatenate(
+            [packed[:, 32 * a : 32 * a + 32], packed[6 * a : 6 * a + 6, 96:128]], axis=0
+        )
+        for t in range(3):
+            in_out[a, t] = whole[8 * t : 8 * t + 8]
 
 
 def local(
@@ -750,7 +764,7 @@
 
     w_in = jnp.transpose(w_in, (0, 1, 3, 2))
     early_size, late_size = 32 // n_group, 16 // n_group
-    raw = (truth_field.shape, (32, 8, LANES), (16, 8, LANES), (24, LANES))
+    raw = (truth_field.shape, (32, 8, LANES), (16, 8, LANES), (18, LANES))
     summed = pl.pallas_call(
         functools.partial(step_kernel, n_group, n_band),
         out_shape=[pltpu.VMEM(shape, F32) for shape in raw],
@@ -818,19 +832,19 @@
             space(F32, n_group, late_size, 8, LANES),
             space(F32, n_band, late_size, 8, LANES),
             space(F32, n_group, late_size, 8, LANES),
-            space(F32, n_group, 24, LANES),
-            space(F32, n_band, 24, LANES),
+            space(F32, n_band, 18, LANES),
+            space(F32, n_group, 18, LANES),
             dma((n_band,)),
             dma((n_band,)),
             dma((4,)),
             dma((4,)),
             dma((2,)),
             dma((2,)),
-            dma((4,)),
-            dma((4,)),
+            dma((4, 2)),
+            dma((4, 2)),
         ]
         + [dma((count,)) for count in (n_group, n_band, n_group) * 2 for _ in range(2)]
-        + [dma((count,)) for count in (n_group, n_band) for _ in range(2)],
+        + [dma((count,)) for count in (n_band, n_group) for _ in range(2)],
         compiler_params=pltpu.CompilerParams(
             collective_id=0, has_side_effects=True, vmem_limit_bytes=VMEM_LIMIT
         ),

time: 57.6 us -> 60.4 us (1.049)
  Pallas kernels: 56.8 us -> 59.6 us
    pallas_call x1, Pallas kernels: 55.8 us -> 58.6 us  [local(): pl.pallas_call(functools.partial(step_kernel, n_group, n_band), out_shape...]
where the time goes in v3:
time: 60.4 us; the launch traced here: 60.3 us
  Pallas kernels  59.6 us (99%)
  between operations  0.65 us (1%)
    pallas_call x1, Pallas kernels, local(): pl.pallas_call(functools.partial(step_kernel, n_group, n_band), out_shape...  58.6 us

profile of v3, /device:TPU:1, one launch (start us, length us, event | category | flops | bytes accessed | tf_op | source)
XLA Modules:
  0.0 60.3 jit_solution(16485983518733123331)
XLA Ops:
  0.6 58.6 %shard_map.163 = (f32[1,4,1440]{2,1,0:T(4,128)S(1)}, f32[32,8,128]{2,1,0:T(8,128)S(1)}, f32[16,8,128]{2,1,0:T(8,128)S(1)}, f32[18,128]{1,0:T(8,128)S(1)}) custom-call(s32[1,24,128]{2,1,0:T(8,128)} %rows_far.1, s32[1,24,128]{2,1,0:T(8,128)} %lons_far.1, f32[1,24,128]{2,1,0:T(8,128)} %obs_far.1, s32[1,24,128]{2,1,0:T(8,128)} %live_far.1, ...), custom_call_target="tpu_custom_call" | custom-call | tf_op jit(solution)/shard_map/pallas_call | solution.py:768
  59.3 1.0 %shard_map.164 = (f32[1,4,1440]{2,1,0:T(4,128)}, f32[3,3,8,32]{3,2,1,0:T(8,128)}, f32[4,4,32,32]{3,2,1,0:T(8,128)}, f32[3,3,32,32]{3,2,1,0:T(8,128)}, f32[3,3,32,64]{3,2,1,0:T(8,128)}, /*index=5*/f32[2,32]{1,0:T(2,128)}) custom-call(f32[1,4,1440]{2,1,0:T(4,128)S(1)} %get-tuple-element.16.mean_ref, f32[32,8,128]{2,1,0:T(8,128)S(1)} %get-tuple-element.17.early_ref, ...), custom_call_target="tpu_custom_call" | custom-call | tf_op jit(solution)/shard_map/pallas_call | solution.py:866

commit v4 on v3

--- a/solution.py
+++ b/solution.py
@@ -20,6 +20,8 @@
 CELL = 120
 SLABS = 12
 CELLS = 92160.0
+FAR_GROUP = (6, 10, 7, 9, 5, 11, 2, 14, 3, 13, 8, 1, 15, 4, 12)
+FAR_BAND = (7, 9, 8, 5, 11, 6, 10, 3, 13, 4, 12, 1, 15, 2, 14)
 VMEM_LIMIT = 56 * 1024 * 1024
 
 
@@ -173,13 +175,13 @@
     g = lax.axis_index("group")
     b = lax.axis_index("band")
     barrier = pltpu.get_barrier_semaphore()
-    for k in range(1, n_group):
+    for k in FAR_BAND:
+        pl.semaphore_signal(
+            barrier, inc=1, device_id=(g, lax.rem(b + k, n_band)), device_id_type=MESH
+        )
+    for k in FAR_GROUP[: n_group - 1]:
         pl.semaphore_signal(
             barrier, inc=1, device_id=(lax.rem(g + k, n_group), b), device_id_type=MESH
-        )
-    for k in range(1, n_band):
-        pl.semaphore_signal(
-            barrier, inc=1, device_id=(g, lax.rem(b + k, n_band)), device_id_type=MESH
         )
 
     def band_peer(k):
@@ -257,7 +259,7 @@
     edge_out[0] = truth_ref[0, 0:1, :]
     edge_out[1] = truth_ref[0, ROWS - 1 : ROWS, :]
     pl.semaphore_wait(barrier, n_group + n_band - 2)
-    for k in range(1, n_band):
+    for k in FAR_BAND:
         peer = band_peer(k)
         send(outbox.at[peer], inbox.at[b], s_a.at[k], r_a.at[b], (g, peer))
     send(edge_out.at[0], edge_in.at[1], s_t.at[0], r_t.at[1], (g, band_peer(-1)))
@@ -299,9 +301,9 @@
     for k in range(1, n_band // 2):
         order += [k, -k]
     order.append(n_band // 2)
-    for quarter in range(4):
+    for first, last in ((0, 5), (5, 10), (10, 14), (14, 16)):
         lefts, rights = [], []
-        for k in order[4 * quarter : 4 * quarter + 4]:
+        for k in order[first:last]:
             peer = band_peer(-k)
             if k:
                 arrive(inbox.at[peer], s_a.at[k % n_band], r_a.at[peer], (g, peer))
@@ -586,7 +588,7 @@
     early[28:32] = jnp.zeros((4, 8, LANES), F32)
 
     def scatter_group(source, size, target, send_sems, recv_sems):
-        for k in range(1, n_group):
+        for k in FAR_GROUP[: n_group - 1]:
             peer = group_peer(k)
             send(
                 source.at[pl.ds(size * peer, size)],
@@ -598,11 +600,11 @@
         target[g] = source[pl.ds(size * g, size)]
 
     def spread_group(target, send_sems, recv_sems):
-        for k in range(1, n_group):
+        for k in FAR_GROUP[: n_group - 1]:
             send(target.at[g], target.at[g], send_sems.at[k], recv_sems.at[g], (group_peer(k), b))
 
     def spread_band(target, send_sems, recv_sems):
-        for k in range(1, n_band):
+        for k in FAR_BAND:
             send(target.at[b], target.at[b], send_sems.at[k], recv_sems.at[b], (g, band_peer(k)))
 
     def await_group(target, send_sems, recv_sems):
@@ -664,9 +666,6 @@
         )
         late[4 * a : 4 * a + 4] = block.reshape(4, 8, LANES)
     scatter_group(late, late_size, late_got, s_l1, r_l1)
-    await_group(early_got, s_e1, r_e1)
-    early_part[b] = added(early_got, n_group)
-    spread_band(early_part, s_e2, r_e2)
     for m in range(4):
         spread_taps(x_gtwo, m, g_two[m], 1)
     value = dot(db_down[...], x_gtwo[...].reshape(384, HALF))
@@ -683,28 +682,31 @@
                 piece = cross[row : row + 24, col : col + 32]
                 total = piece if total is None else total + piece
         in_grads.append(total)
-    in_got[b] = jnp.concatenate(
+    in_got[g] = jnp.concatenate(
         [
             jnp.concatenate([grad[:18] for grad in in_grads], axis=1),
             jnp.concatenate([grad[18:] for grad in in_grads], axis=0),
         ],
         axis=1,
     )
-    spread_band(in_got, s_i1, r_i1)
+    spread_group(in_got, s_i1, r_i1)
+    await_group(early_got, s_e1, r_e1)
+    early_part[b] = added(early_got, n_group)
+    spread_band(early_part, s_e2, r_e2)
     await_group(late_got, s_l1, r_l1)
     late_part[b] = added(late_got, n_group)
     spread_band(late_part, s_l2, r_l2)
-    await_band(in_got, s_i1, r_i1)
-    in_part[g] = added(in_got, n_band)
-    spread_group(in_part, s_i2, r_i2)
+    await_group(in_got, s_i1, r_i1)
+    in_part[b] = added(in_got, n_group)
+    spread_band(in_part, s_i2, r_i2)
     await_band(early_part, s_e2, r_e2)
     early_full[g] = added(early_part, n_band)
     spread_group(early_full, s_e3, r_e3)
     await_band(late_part, s_l2, r_l2)
     late_full[g] = added(late_part, n_band)
     spread_group(late_full, s_l3, r_l3)
-    await_group(in_part, s_i2, r_i2)
-    in_out[...] = added(in_part, n_group)
+    await_band(in_part, s_i2, r_i2)
+    in_out[...] = added(in_part, n_band)
     await_group(early_full, s_e3, r_e3)
     early_out[...] = early_full[...].reshape(32, 8, LANES)
     await_group(late_full, s_l3, r_l3)
@@ -832,8 +834,8 @@
             space(F32, n_group, late_size, 8, LANES),
             space(F32, n_band, late_size, 8, LANES),
             space(F32, n_group, late_size, 8, LANES),
+            space(F32, n_group, 18, LANES),
             space(F32, n_band, 18, LANES),
-            space(F32, n_group, 18, LANES),
             dma((n_band,)),
             dma((n_band,)),
             dma((4,)),
@@ -844,7 +846,7 @@
             dma((4, 2)),
         ]
         + [dma((count,)) for count in (n_group, n_band, n_group) * 2 for _ in range(2)]
-        + [dma((count,)) for count in (n_band, n_group) for _ in range(2)],
+        + [dma((count,)) for count in (n_group, n_band) for _ in range(2)],
         compiler_params=pltpu.CompilerParams(
             collective_id=0, has_side_effects=True, vmem_limit_bytes=VMEM_LIMIT
         ),

time: 60.4 us -> 56.8 us (0.940)
  Pallas kernels: 59.6 us -> 56 us
    pallas_call x1, Pallas kernels: 58.6 us -> 55 us  [local(): pl.pallas_call(functools.partial(step_kernel, n_group, n_band), out_shape...]
where the time goes in v4:
time: 56.8 us; the launch traced here: 56.7 us
  Pallas kernels  56 us (99%)
  between operations  0.65 us (1%)
    pallas_call x1, Pallas kernels, local(): pl.pallas_call(functools.partial(step_kernel, n_group, n_band), out_shape...  55 us

profile of v4, /device:TPU:1, one launch (start us, length us, event | category | flops | bytes accessed | tf_op | source)
XLA Modules:
  0.0 56.7 jit_solution(15347426753162451556)
XLA Ops:
  0.6 55.0 %shard_map.163 = (f32[1,4,1440]{2,1,0:T(4,128)S(1)}, f32[32,8,128]{2,1,0:T(8,128)S(1)}, f32[16,8,128]{2,1,0:T(8,128)S(1)}, f32[18,128]{1,0:T(8,128)S(1)}) custom-call(s32[1,24,128]{2,1,0:T(8,128)} %rows_far.1, s32[1,24,128]{2,1,0:T(8,128)} %lons_far.1, f32[1,24,128]{2,1,0:T(8,128)} %obs_far.1, s32[1,24,128]{2,1,0:T(8,128)} %live_far.1, ...), custom_call_target="tpu_custom_call" | custom-call | tf_op jit(solution)/shard_map/pallas_call | solution.py:770
  55.7 1.0 %shard_map.164 = (f32[1,4,1440]{2,1,0:T(4,128)}, f32[3,3,8,32]{3,2,1,0:T(8,128)}, f32[4,4,32,32]{3,2,1,0:T(8,128)}, f32[3,3,32,32]{3,2,1,0:T(8,128)}, f32[3,3,32,64]{3,2,1,0:T(8,128)}, /*index=5*/f32[2,32]{1,0:T(2,128)}) custom-call(f32[1,4,1440]{2,1,0:T(4,128)S(1)} %get-tuple-element.16.mean_ref, f32[32,8,128]{2,1,0:T(8,128)S(1)} %get-tuple-element.17.early_ref, ...), custom_call_target="tpu_custom_call" | custom-call | tf_op jit(solution)/shard_map/pallas_call | solution.py:868

commit v5 on v4

--- a/solution.py
+++ b/solution.py
@@ -88,7 +88,6 @@
     mean_out,
     early_out,
     late_out,
-    in_out,
     rows_ref,
     lons_ref,
     obs_ref,
@@ -145,8 +144,6 @@
     late_got,
     late_part,
     late_full,
-    in_got,
-    in_part,
     s_a,
     r_a,
     s_f,
@@ -167,10 +164,6 @@
     r_l2,
     s_l3,
     r_l3,
-    s_i1,
-    r_i1,
-    s_i2,
-    r_i2,
 ):
     g = lax.axis_index("group")
     b = lax.axis_index("band")
@@ -392,7 +385,8 @@
                     wb_up3[row : row + 32, col : col + 32] = upper
                     wb_up1[row : row + 32, col : col + 32] = lower
                     db_up[2 * row : 2 * row + 64, col : col + 32] = turned_up[:, at : at + 32]
-                row, col = i * 32, (i + 2 * a) * 96 + t * 32
+            for m in range(4):
+                row, col = m * 32, (m + 2 * a) * 96 + t * 32
                 wb_mid[row : row + 32, col : col + 32] = w_mid[a, t]
                 db_mid[row : row + 32, col : col + 32] = turned_mid[:, at : at + 32]
     for a in range(4):
@@ -481,21 +475,19 @@
 
     lax.fori_loop(0, 4, two_step, 0, unroll=True)
 
-    for it in range(2):
-        value = dot(wb_mid[...], x_two[2 * it : 2 * it + 6].reshape(576, HALF))
-        for m in range(2):
-            row = 2 * it + m
-            place = 2 * b + row - 1
-            inside = as_scale(jnp.logical_and(place >= 0, place < 2 * n_band))
-            here = value[32 * m : 32 * m + 32]
-            pre_three[row] = here
-            hidden = (here * sigmoid(here) * inside).astype(BF16)
-            before, after = later(hidden, 1), earlier(hidden, 1)
-            for target in (2 * row, 2 * row + 1):
-                x_three[target, 0:32] = before
-                x_three[target, 32:64] = hidden
-                x_three[target, 64:96] = hidden
-                x_three[target, 96:128] = after
+    value = dot(wb_mid[...], x_two[...].reshape(768, HALF))
+    for row in range(4):
+        place = 2 * b + row - 1
+        inside = as_scale(jnp.logical_and(place >= 0, place < 2 * n_band))
+        here = value[32 * row : 32 * row + 32]
+        pre_three[row] = here
+        hidden = (here * sigmoid(here) * inside).astype(BF16)
+        before, after = later(hidden, 1), earlier(hidden, 1)
+        for target in (2 * row, 2 * row + 1):
+            x_three[target, 0:32] = before
+            x_three[target, 32:64] = hidden
+            x_three[target, 64:96] = hidden
+            x_three[target, 96:128] = after
 
     def four_step(it, carry):
         value = dot(wb_up3[...], x_three[pl.ds(2 * it, 4)].reshape(512, HALF))
@@ -623,7 +615,7 @@
             total = total + ref[n]
         return total
 
-    early_size, late_size = 32 // n_group, 16 // n_group
+    early_size = 32 // n_group
     scatter_group(early, early_size, early_got, s_e1, r_e1)
 
     cuts = thirds(jnp.concatenate([mean, jnp.zeros((16, 48), F32)], axis=1))
@@ -651,21 +643,19 @@
         there = as_scale(jnp.logical_and(b + k >= 0, b + k < n_band))
         value = (far_three[n, m].astype(F32) * there).astype(BF16)
         spread_taps(x_gthree, 3 + 2 * k + m, value, 2)
-    for it in range(2):
-        value = dot(db_mid[...], x_gthree[2 * it : 2 * it + 6].reshape(576, HALF))
-        for m in range(2):
-            row = 2 * it + m
-            place = 2 * b + row - 1
-            inside = as_scale(jnp.logical_and(place >= 0, place < 2 * n_band))
-            here = value[32 * m : 32 * m + 32] * slope(pre_two[2 + row]) * inside
-            g_two[row] = here.astype(BF16)
+    value = dot(db_mid[...], x_gthree[...].reshape(768, HALF))
+    for row in range(4):
+        place = 2 * b + row - 1
+        inside = as_scale(jnp.logical_and(place >= 0, place < 2 * n_band))
+        here = value[32 * row : 32 * row + 32] * slope(pre_two[2 + row]) * inside
+        g_two[row] = here.astype(BF16)
     cross = dot_t(g_two[1:3].reshape(64, HALF), x_one[6:12].reshape(768, HALF))
+    down_grads = []
     for a in range(4):
         block = (
             cross[0:32, 128 * a : 128 * a + 128] + cross[32:64, 128 * a + 256 : 128 * a + 384]
         )
-        late[4 * a : 4 * a + 4] = block.reshape(4, 8, LANES)
-    scatter_group(late, late_size, late_got, s_l1, r_l1)
+        down_grads.append(block)
     for m in range(4):
         spread_taps(x_gtwo, m, g_two[m], 1)
     value = dot(db_down[...], x_gtwo[...].reshape(384, HALF))
@@ -682,48 +672,51 @@
                 piece = cross[row : row + 24, col : col + 32]
                 total = piece if total is None else total + piece
         in_grads.append(total)
-    in_got[g] = jnp.concatenate(
+    in_block = jnp.concatenate(
         [
             jnp.concatenate([grad[:18] for grad in in_grads], axis=1),
             jnp.concatenate([grad[18:] for grad in in_grads], axis=0),
         ],
         axis=1,
     )
-    spread_group(in_got, s_i1, r_i1)
+    lines = jnp.concatenate(down_grads + [in_block, jnp.zeros((14, LANES), F32)], axis=0)
+    rows = 160 // n_group
+    for n in range(n_group):
+        late[n] = lines[rows * n : rows * n + rows]
+    for k in FAR_GROUP[: n_group - 1]:
+        peer = group_peer(k)
+        send(late.at[peer], late_got.at[g], s_l1.at[k], r_l1.at[g], (peer, b))
+    late_got[g] = late[g]
     await_group(early_got, s_e1, r_e1)
     early_part[b] = added(early_got, n_group)
     spread_band(early_part, s_e2, r_e2)
     await_group(late_got, s_l1, r_l1)
     late_part[b] = added(late_got, n_group)
     spread_band(late_part, s_l2, r_l2)
-    await_group(in_got, s_i1, r_i1)
-    in_part[b] = added(in_got, n_group)
-    spread_band(in_part, s_i2, r_i2)
     await_band(early_part, s_e2, r_e2)
     early_full[g] = added(early_part, n_band)
     spread_group(early_full, s_e3, r_e3)
     await_band(late_part, s_l2, r_l2)
     late_full[g] = added(late_part, n_band)
     spread_group(late_full, s_l3, r_l3)
-    await_band(in_part, s_i2, r_i2)
-    in_out[...] = added(in_part, n_band)
     await_group(early_full, s_e3, r_e3)
     early_out[...] = early_full[...].reshape(32, 8, LANES)
     await_group(late_full, s_l3, r_l3)
-    late_out[...] = late_full[...].reshape(16, 8, LANES)
+    late_out[...] = late_full[...]
     for copy in sent:
         copy.wait_send()
 
 
 def outputs_kernel(
-    mean_ref, early_ref, late_ref, in_ref, mean_out, in_out, down_out, mid_out, up_out, head_out
+    mean_ref, early_ref, late_ref, mean_out, in_out, down_out, mid_out, up_out, head_out
 ):
     mean_out[...] = mean_ref[...]
     early = [early_ref[4 * n : 4 * n + 4].reshape(32, LANES) for n in range(7)]
     pieces = [early[n][:, 96:128] for n in range(6)]
     pieces += [early[6][:, 32 * t : 32 * t + 32] for t in range(3)]
+    lines = jnp.concatenate([late_ref[n] for n in range(late_ref.shape[0])], axis=0)
     for a in range(4):
-        block = late_ref[4 * a : 4 * a + 4].reshape(32, LANES)
+        block = lines[32 * a : 32 * a + 32]
         for t in range(4):
             down_out[a, t] = block[:, 32 * t : 32 * t + 32]
     for a in range(3):
@@ -733,7 +726,7 @@
             )
             mid_out[a, t] = pieces[3 * a + t]
     head_out[...] = early[6][0:2, 96:128]
-    packed = in_ref[...]
+    packed = lines[128:146]
     for a in range(3):
         whole = jnp.concatenate(
             [packed[:, 32 * a : 32 * a + 32], packed[6 * a : 6 * a + 6, 96:128]], axis=0
@@ -765,13 +758,13 @@
         return pltpu.VMEM(shape, dtype)
 
     w_in = jnp.transpose(w_in, (0, 1, 3, 2))
-    early_size, late_size = 32 // n_group, 16 // n_group
-    raw = (truth_field.shape, (32, 8, LANES), (16, 8, LANES), (18, LANES))
+    early_size, late_size = 32 // n_group, 160 // n_group
+    raw = (truth_field.shape, (32, 8, LANES), (n_group, late_size, LANES))
     summed = pl.pallas_call(
         functools.partial(step_kernel, n_group, n_band),
         out_shape=[pltpu.VMEM(shape, F32) for shape in raw],
         in_specs=[pl.BlockSpec(memory_space=pl.ANY)] * 10 + [smem] * 2,
-        out_specs=[vmem] * 4,
+        out_specs=[vmem] * 3,
         scratch_shapes=[
             pltpu.VMEM(part.shape, part.dtype)
             for part in (
@@ -820,22 +813,20 @@
             space(BF16, 4, 64, HALF),
             space(BF16, 192, 160),
             space(BF16, 64, 768),
-            space(BF16, 64, 576),
+            space(BF16, 128, 768),
             space(BF16, 128, 512),
             space(BF16, 128, 512),
             space(BF16, 256, 512),
-            space(BF16, 64, 576),
+            space(BF16, 128, 768),
             space(BF16, 256, 384),
             space(F32, 32, 8, LANES),
             space(F32, n_group, early_size, 8, LANES),
             space(F32, n_band, early_size, 8, LANES),
             space(F32, n_group, early_size, 8, LANES),
-            space(F32, 16, 8, LANES),
-            space(F32, n_group, late_size, 8, LANES),
-            space(F32, n_band, late_size, 8, LANES),
-            space(F32, n_group, late_size, 8, LANES),
-            space(F32, n_group, 18, LANES),
-            space(F32, n_band, 18, LANES),
+            space(F32, n_group, late_size, LANES),
+            space(F32, n_group, late_size, LANES),
+            space(F32, n_band, late_size, LANES),
+            space(F32, n_group, late_size, LANES),
             dma((n_band,)),
             dma((n_band,)),
             dma((4,)),
@@ -845,8 +836,7 @@
             dma((4, 2)),
             dma((4, 2)),
         ]
-        + [dma((count,)) for count in (n_group, n_band, n_group) * 2 for _ in range(2)]
-        + [dma((count,)) for count in (n_group, n_band) for _ in range(2)],
+        + [dma((count,)) for count in (n_group, n_band, n_group) * 2 for _ in range(2)],
         compiler_params=pltpu.CompilerParams(
             collective_id=0, has_side_effects=True, vmem_limit_bytes=VMEM_LIMIT
         ),
@@ -868,7 +858,7 @@
     mean, grad_in, grad_down, grad_mid, grad_up, grad_head = pl.pallas_call(
         outputs_kernel,
         out_shape=[jax.ShapeDtypeStruct(out.shape, F32) for out in outs],
-        in_specs=[vmem] * 4,
+        in_specs=[vmem] * 3,
         out_specs=[vmem] * 6,
     )(*[pltpu.with_memory_space_constraint(part, pltpu.VMEM) for part in summed])
     return mean, jnp.transpose(grad_in, (0, 1, 3, 2)), grad_down, grad_mid, grad_up, grad_head

time: 56.8 us -> 56.9 us (level)
  no operation moved by 1% of the time
where the time goes in v5:
time: 56.9 us; the launch traced here: 56.7 us
  Pallas kernels  56.1 us (99%)
  between operations  0.64 us (1%)
    pallas_call x1, Pallas kernels, local(): pl.pallas_call(functools.partial(step_kernel, n_group, n_band), out_shape...  55 us

profile of v5, /device:TPU:1, one launch (start us, length us, event | category | flops | bytes accessed | tf_op | source)
XLA Modules:
  0.0 56.7 jit_solution(241424368966077482)
XLA Ops:
  0.6 55.0 %shard_map.163 = (f32[1,4,1440]{2,1,0:T(4,128)S(1)}, f32[32,8,128]{2,1,0:T(8,128)S(1)}, f32[16,10,128]{2,1,0:T(8,128)S(1)}) custom-call(s32[1,24,128]{2,1,0:T(8,128)} %rows_far.1, s32[1,24,128]{2,1,0:T(8,128)} %lons_far.1, f32[1,24,128]{2,1,0:T(8,128)} %obs_far.1, s32[1,24,128]{2,1,0:T(8,128)} %live_far.1, f32[1,4,1440]{2,1,0:T(4,128)} %truth_far.1, ...), custom_call_target="tpu_custom_call" | custom-call | tf_op jit(solution)/shard_map/pallas_call | solution.py:763
  55.7 1.0 %shard_map.164 = (f32[1,4,1440]{2,1,0:T(4,128)}, f32[3,3,8,32]{3,2,1,0:T(8,128)}, f32[4,4,32,32]{3,2,1,0:T(8,128)}, f32[3,3,32,32]{3,2,1,0:T(8,128)}, f32[3,3,32,64]{3,2,1,0:T(8,128)}, /*index=5*/f32[2,32]{1,0:T(2,128)}) custom-call(f32[1,4,1440]{2,1,0:T(4,128)S(1)} %get-tuple-element.15.mean_ref, f32[32,8,128]{2,1,0:T(8,128)S(1)} %get-tuple-element.16.early_ref, ...), custom_call_target="tpu_custom_call" | custom-call | tf_op jit(solution)/shard_map/pallas_call | solution.py:858
